TPU v7x, 512 devices: a whole 4x8x8 slice. The times are simulated.
512 devices in a mesh: gx: 64 (over x, y, core), gy: 8 (over z).
Axes of the slice: x: 4, y: 8, z: 8, core: 2. Of those that a mesh axis runs over, the one named last changes fastest.
Arguments:
- magnetization: float32 [3, 1024, 128, 512], P(None, 'gx', 'gy'), may hold values from -2.2 to 2.2
- easy_axes: float32 [3, 1024, 128, 512], P(None, 'gx', 'gy'), may hold values from -6 to 6
- pins: float32 [2, 3, 128, 512], P(None, None, 'gy'), may hold values from -4 to 4
Outputs:
- final_field: float32 [3, 1024, 128, 512], P(None, 'gx', 'gy')
All inputs are finite; a program needn't handle non-finite values.
Results may differ from a plain program's by a relative error of at most 0.0003.
Values sent between devices are 32-bit elements; how exact they have to be, the bound alone decides.
A program may use at most 64 MiB of HBM per device.

v0:
```python
import jax
import jax.numpy as jnp
import numpy as np
from jax import lax
from jax.sharding import Mesh
from jax.sharding import PartitionSpec as P

STEPS = 2
GX = ("gx_0", "gx_1", "gx_2")


diffusion = 4000.0
anisotropy_rate = 0.3
torque_rate = 0.2
exchange_rate = 0.1
norm_floor = 0.5


def neutral_like(array, identity):
    return jax.tree.map(
        lambda part, zero: jnp.zeros_like(part) + jnp.asarray(zero, part.dtype), array, identity
    )


def entering(array, axes, combine, identity, reverse):
    before = start = neutral_like(array, identity)
    total = array
    for axis in reversed(axes):
        size, mine = (lax.axis_size(axis), lax.axis_index(axis))
        pieces = jax.tree.map(lambda part: lax.all_gather(part, axis), total)
        inside, total = (start, start)
        for k in reversed(range(size)) if reverse else range(size):
            passed = k > mine if reverse else k < mine
            total = combine(total, jax.tree.map(lambda part: part[k], pieces))
            inside = jax.tree.map(lambda new, old: jnp.where(passed, new, old), total, inside)
        before = combine(inside, before)
    return before


def with_halo(block, sides, width):
    for axis, dim in sides:
        count = lax.axis_size(axis)
        forward = [(i, i + 1) for i in range(count - 1)]
        forward.append((count - 1, 0))
        backward = [(target, source) for source, target in forward]
        low = lax.ppermute(
            lax.slice_in_dim(block, block.shape[dim] - width, None, axis=dim), axis, forward
        )
        high = lax.ppermute(lax.slice_in_dim(block, 0, width, axis=dim), axis, backward)
        block = jnp.concatenate([low, block, high], axis=dim)
    return block


def block_inverse(inner_count):
    leading = 1.0 + 2.0 * diffusion
    theta = [1.0, leading]
    for index in range(2, inner_count + 1):
        theta.append(leading * theta[index - 1] - diffusion * diffusion * theta[index - 2])
    inverse = np.zeros((inner_count, inner_count))
    for row in range(inner_count):
        for column in range(inner_count):
            small = min(row, column)
            large = max(row, column)
            inverse[row, column] = (
                diffusion ** (large - small)
                * theta[small]
                * theta[inner_count - 1 - large]
                / theta[inner_count]
            )
    return inverse


def interface_tables(planes, groups):
    inner_count = planes - 2
    inverse = block_inverse(inner_count)
    diagonal = 1.0 + 2.0 * diffusion - diffusion * diffusion * inverse[0, 0]
    within = -diffusion * diffusion * inverse[0, inner_count - 1]
    count = 2 * groups
    numbers = np.arange(count)
    lower_band = np.where(numbers % 2 == 1, within, -diffusion)
    lower_band[0] = 0.0
    upper_band = np.where(numbers % 2 == 0, within, -diffusion)
    upper_band[count - 1] = 0.0
    middle = np.full(count, diagonal)
    pivots = np.zeros(count)
    pivots[0] = middle[0]
    for index in range(1, count):
        pivots[index] = (
            middle[index] - lower_band[index] * upper_band[index - 1] / pivots[index - 1]
        )
    factors = np.zeros(count)
    factors[1:] = lower_band[1:] / pivots[:-1]
    return (inverse, lower_band, middle, upper_band, pivots, factors)


def compose(earlier, later):
    return (earlier[0] * later[0], later[0] * earlier[1] + later[1])


def per_device(magnetization, easy_axes, pins):
    planes = magnetization.shape[1]
    groups = lax.axis_size(GX)
    position = lax.axis_index(GX)
    inverse, lower_band, middle, upper_band, pivots, factors = interface_tables(planes, groups)
    inverse_here = jnp.asarray(inverse, jnp.float32)
    edge_first = diffusion * inverse_here[:, 0:1]
    edge_last = diffusion * inverse_here[:, -1:]
    upper_here = jnp.asarray(upper_band, jnp.float32)
    pivot_table = jnp.asarray(pivots, jnp.float32)
    factor_table = jnp.asarray(factors, jnp.float32)
    is_first = (position == 0).astype(jnp.float32)
    is_last = (position == groups - 1).astype(jnp.float32)
    field = magnetization
    for stepno in range(STEPS):
        for component in range(3):
            projection = jnp.sum(field * easy_axes, axis=0)
            source = field[component] + anisotropy_rate * projection * easy_axes[component]
            source = source.at[0].add(diffusion * is_first * pins[0, component])
            source = source.at[-1].add(diffusion * is_last * pins[1, component])
            columns = source.reshape(planes, -1)
            inner = jnp.dot(
                inverse_here,
                columns[1:-1],
                precision=lax.Precision.HIGHEST,
                preferred_element_type=jnp.float32,
            )
            reduced = jnp.stack(
                [columns[0] + diffusion * inner[0], columns[-1] + diffusion * inner[-1]]
            )
            factor_pair = lax.dynamic_slice(factor_table, (2 * position,), (2,))
            pivot_pair = lax.dynamic_slice(pivot_table, (2 * position,), (2,))
            upper_pair = lax.dynamic_slice(upper_here, (2 * position,), (2,))
            start_maps = (jnp.ones((1,), jnp.float32), jnp.zeros_like(reduced[0]))
            slope = (factor_pair[1] * factor_pair[0]).reshape(1)
            offset = reduced[1] - factor_pair[1] * reduced[0]
            prior = entering((slope, offset), GX, compose, start_maps, False)
            eliminated_first = reduced[0] - factor_pair[0] * prior[1]
            eliminated_last = reduced[1] - factor_pair[1] * eliminated_first
            scaled_first = eliminated_first / pivot_pair[0]
            scaled_last = eliminated_last / pivot_pair[1]
            ratio_first = upper_pair[0] / pivot_pair[0]
            ratio_last = upper_pair[1] / pivot_pair[1]
            back_slope = (ratio_first * ratio_last).reshape(1)
            back_offset = scaled_first - ratio_first * scaled_last
            later = entering((back_slope, back_offset), GX, compose, start_maps, True)
            last_value = scaled_last - ratio_last * later[1]
            first_value = scaled_first - ratio_first * last_value
            boundary = jnp.stack([first_value, last_value])
            middle_rows = inner + edge_first * boundary[0:1] + edge_last * boundary[1:2]
            field = field.at[component].set(
                jnp.concatenate([boundary[0:1], middle_rows, boundary[1:2]], axis=0).reshape(
                    source.shape
                )
            )
        projection = jnp.sum(field * easy_axes, axis=0)
        padded = with_halo(field, (("gy", 2),), 1)
        neighbours = (
            padded[:, :, 2:] + padded[:, :, :-2] + jnp.roll(field, 1, 3) + jnp.roll(field, -1, 3)
        )
        effective = exchange_rate * (neighbours - 4.0 * field) + projection[None] * easy_axes
        twisted = jnp.cross(field, effective, axis=0)
        rotated = field - torque_rate * twisted
        length = jnp.sqrt(jnp.sum(rotated * rotated, axis=0))
        field = rotated / jnp.maximum(length, norm_floor)[None]
    return field


def solution(mesh):
    split = Mesh(mesh.devices.reshape(4, 8, 2, mesh.shape["gy"]), ("gx_0", "gx_1", "gx_2", "gy"))
    in_specs = (P(None, GX, "gy", None), P(None, GX, "gy", None), P(None, None, "gy", None))
    out_specs = P(None, GX, "gy", None)
    return jax.shard_map(
        per_device, mesh=split, in_specs=in_specs, out_specs=out_specs, check_vma=False
    )
```

profile of v0, /device:TPU:4, one launch (start us, length us, event | category | flops | bytes accessed | tf_op | source)
XLA Modules:
  0.0 739.7 jit_solution(492890243293233989)
XLA Ops:
  17.3 17.6 %all-reduce.6 = (f32[8]{0:T(128)S(1)}, f32[8]{0:T(128)S(1)}) all-reduce(f32[8]{0:T(128)S(1)} %dynamic-update-slice.55, f32[8]{0:T(128)S(1)} %dynamic-update-slice.58), channel_id=2, replica_groups=mesh['gx_0'=4,'gx_1'=8,'gx_2'=2,'gy'=8] {'gx_1'}, use_global_device_ids=true, to_apply=%add.1 | all-reduce | flops 16 | bytes 128
  52.3 24.8 %all-gather.5 = f32[8,1,8192]{2,1,0:T(1,128)S(1)} all-gather(f32[1,1,8192]{2,1,0:T(1,128)S(1)} %slice_add_fusion.80), channel_id=1, replica_groups=mesh['gx_0'=4,'gx_1'=8,'gx_2'=2,'gy'=8] {'gx_1'}, dimensions={0}, use_global_device_ids=true | all-gather | bytes 294912 | tf_op jit(solution)/shard_map/all_gather | solution.py:30
  77.1 5.1 fusion.239
  82.2 13.0 %all-gather.6 = f32[4,1,8192]{2,1,0:T(1,128)} all-gather(f32[1,1,8192]{2,1,0:T(1,128)S(1)} %bitcast.1662), channel_id=1, replica_groups=mesh['gx_0'=4,'gx_1'=8,'gx_2'=2,'gy'=8] {'gx_0'}, dimensions={0}, use_global_device_ids=true | all-gather | bytes 163840 | tf_op jit(solution)/shard_map/all_gather | solution.py:30
  103.2 8.6 %all-reduce.7 = (f32[4]{0:T(128)}, f32[4]{0:T(128)}) all-reduce(f32[4]{0:T(128)} %dynamic-update-slice.56, f32[4]{0:T(128)} %dynamic-update-slice.59), channel_id=3, replica_groups=mesh['gx_0'=4,'gx_1'=8,'gx_2'=2,'gy'=8] {'gx_0'}, use_global_device_ids=true, to_apply=%add.2 | all-reduce | flops 8 | bytes 64
  118.8 8.9 %subtract_bitcast_fusion.16 = (f32[1,1,8192]{2,1,0:T(1,128)S(1)}, f32[1,8192]{1,0:T(1,128)S(1)}, f32[1,8192]{1,0:T(1,128)S(1)}) fusion(f32[]{:T(128)S(6)} %div.116, f32[]{:T(128)} %bitcast.52, f32[]{:T(128)} %bitcast.54, f32[]{:T(128)} %bitcast.5, f32[1,8192]{1,0:T(1,128)} %bitcast.1677, f32[14,8192]{1,0:T(8,128)} %copy-done.1, ...), kind=kLoop, calls=%fused_computation.701 | loop fusion | flops 401408 | bytes 688214
  130.2 24.8 %all-gather.8 = f32[8,1,8192]{2,1,0:T(1,128)S(1)} all-gather(f32[1,1,8192]{2,1,0:T(1,128)S(1)} %slice_add_fusion.74), channel_id=1, replica_groups=mesh['gx_0'=4,'gx_1'=8,'gx_2'=2,'gy'=8] {'gx_1'}, dimensions={0}, use_global_device_ids=true | all-gather | bytes 294912 | tf_op jit(solution)/shard_map/all_gather | solution.py:30
  155.0 4.4 fusion.229
  159.4 12.6 %all-gather.9 = f32[4,1,8192]{2,1,0:T(1,128)S(1)} all-gather(f32[1,1,8192]{2,1,0:T(1,128)S(1)} %bitcast.1663), channel_id=1, replica_groups=mesh['gx_0'=4,'gx_1'=8,'gx_2'=2,'gy'=8] {'gx_0'}, dimensions={0}, use_global_device_ids=true | all-gather | bytes 163840 | tf_op jit(solution)/shard_map/all_gather | solution.py:30
  178.4 5.4 multiply_subtract_fusion.15
  190.0 24.8 %all-gather.11 = f32[8,1,8192]{2,1,0:T(1,128)S(1)} all-gather(f32[1,1,8192]{2,1,0:T(1,128)S(1)} %slice_add_fusion.66), channel_id=1, replica_groups=mesh['gx_0'=4,'gx_1'=8,'gx_2'=2,'gy'=8] {'gx_1'}, dimensions={0}, use_global_device_ids=true | all-gather | bytes 294912 | tf_op jit(solution)/shard_map/all_gather | solution.py:30
  214.8 4.5 fusion.215
  219.3 12.0 %all-gather.12 = f32[4,1,8192]{2,1,0:T(1,128)S(1)} all-gather(f32[1,1,8192]{2,1,0:T(1,128)S(1)} %bitcast.1666), channel_id=1, replica_groups=mesh['gx_0'=4,'gx_1'=8,'gx_2'=2,'gy'=8] {'gx_0'}, dimensions={0}, use_global_device_ids=true | all-gather | bytes 163840 | tf_op jit(solution)/shard_map/all_gather | solution.py:30
  231.3 7.7 %subtract_bitcast_fusion.14 = (f32[1,1,8192]{2,1,0:T(1,128)S(1)}, f32[1,8192]{1,0:T(1,128)S(1)}, f32[1,8192]{1,0:T(1,128)S(1)}) fusion(f32[]{:T(128)S(6)} %div.116, f32[]{:T(128)} %bitcast.52, f32[]{:T(128)} %bitcast.54, f32[]{:T(128)} %bitcast.5, f32[1,8192]{1,0:T(1,128)S(1)} %bitcast.1697, f32[14,8192]{1,0:T(8,128)S(1)} %fusion.288, ...), kind=kLoop, calls=%fused_computation.693 | loop fusion | flops 401408 | bytes 688214
  241.5 24.9 %all-gather.14 = f32[8,1,8192]{2,1,0:T(1,128)S(1)} all-gather(f32[1,1,8192]{2,1,0:T(1,128)S(1)} %slice_add_fusion.60), channel_id=1, replica_groups=mesh['gx_0'=4,'gx_1'=8,'gx_2'=2,'gy'=8] {'gx_1'}, dimensions={0}, use_global_device_ids=true | all-gather | bytes 294912 | tf_op jit(solution)/shard_map/all_gather | solution.py:30
  270.9 12.2 %all-gather.15 = f32[4,1,8192]{2,1,0:T(1,128)S(1)} all-gather(f32[1,1,8192]{2,1,0:T(1,128)S(1)} %bitcast.1667), channel_id=1, replica_groups=mesh['gx_0'=4,'gx_1'=8,'gx_2'=2,'gy'=8] {'gx_0'}, dimensions={0}, use_global_device_ids=true | all-gather | bytes 163840 | tf_op jit(solution)/shard_map/all_gather | solution.py:30
  283.0 5.4 multiply_subtract_fusion.12
  293.8 25.0 %all-gather.17 = f32[8,1,8192]{2,1,0:T(1,128)S(1)} all-gather(f32[1,1,8192]{2,1,0:T(1,128)S(1)} %slice_add_fusion.52), channel_id=1, replica_groups=mesh['gx_0'=4,'gx_1'=8,'gx_2'=2,'gy'=8] {'gx_1'}, dimensions={0}, use_global_device_ids=true | all-gather | bytes 294912 | tf_op jit(solution)/shard_map/all_gather | solution.py:30
  318.8 4.5 fusion.191
  323.2 12.0 %all-gather.18 = f32[4,1,8192]{2,1,0:T(1,128)S(1)} all-gather(f32[1,1,8192]{2,1,0:T(1,128)S(1)} %bitcast.1668), channel_id=1, replica_groups=mesh['gx_0'=4,'gx_1'=8,'gx_2'=2,'gy'=8] {'gx_0'}, dimensions={0}, use_global_device_ids=true | all-gather | bytes 163840 | tf_op jit(solution)/shard_map/all_gather | solution.py:30
  335.2 7.7 %subtract_bitcast_fusion.12 = (f32[1,1,8192]{2,1,0:T(1,128)S(1)}, f32[1,8192]{1,0:T(1,128)S(1)}, f32[1,8192]{1,0:T(1,128)S(1)}) fusion(f32[]{:T(128)S(6)} %div.116, f32[]{:T(128)} %bitcast.52, f32[]{:T(128)} %bitcast.54, f32[]{:T(128)} %bitcast.5, f32[1,8192]{1,0:T(1,128)S(1)} %bitcast.1701, f32[14,8192]{1,0:T(8,128)S(1)} %fusion.289, ...), kind=kLoop, calls=%fused_computation.685 | loop fusion | flops 401408 | bytes 688214
  345.5 24.8 %all-gather.20 = f32[8,1,8192]{2,1,0:T(1,128)S(1)} all-gather(f32[1,1,8192]{2,1,0:T(1,128)S(1)} %slice_add_fusion.46), channel_id=1, replica_groups=mesh['gx_0'=4,'gx_1'=8,'gx_2'=2,'gy'=8] {'gx_1'}, dimensions={0}, use_global_device_ids=true | all-gather | bytes 294912 | tf_op jit(solution)/shard_map/all_gather | solution.py:30
  374.7 12.0 %all-gather.21 = f32[4,1,8192]{2,1,0:T(1,128)S(1)} all-gather(f32[1,1,8192]{2,1,0:T(1,128)S(1)} %bitcast.1669), channel_id=1, replica_groups=mesh['gx_0'=4,'gx_1'=8,'gx_2'=2,'gy'=8] {'gx_0'}, dimensions={0}, use_global_device_ids=true | all-gather | bytes 163840 | tf_op jit(solution)/shard_map/all_gather | solution.py:30
  386.7 5.4 multiply_subtract_fusion.9
  392.9 10.6 %collective-permute-start = (f32[3,16,1,512]{3,2,1,0:T(1,128)S(1)}, f32[3,16,1,512]{3,2,1,0:T(1,128)S(1)}, u32[]{:S(2)}, u32[]{:S(2)}) collective-permute-start(f32[3,16,1,512]{3,2,1,0:T(1,128)S(1)} %get-tuple-element.312), channel_id=1, source_target_pairs={{1,0},{2,1},{3,2},{4,3},{5,4},{6,5},{7,6},{0,7},{9,8},{10,9},{11,1... | collective-permute-start | bytes 294920 | tf_op jit(solution)/shard_map/ppermute | solution.py:49
  406.7 4.6 collective-permute-done.1
  418.7 24.8 %all-gather.23 = f32[8,1,8192]{2,1,0:T(1,128)S(1)} all-gather(f32[1,1,8192]{2,1,0:T(1,128)S(1)} %slice_add_fusion.38), channel_id=1, replica_groups=mesh['gx_0'=4,'gx_1'=8,'gx_2'=2,'gy'=8] {'gx_1'}, dimensions={0}, use_global_device_ids=true | all-gather | bytes 294912 | tf_op jit(solution)/shard_map/all_gather | solution.py:30
  443.5 4.5 fusion.167
  447.9 12.2 %all-gather.24 = f32[4,1,8192]{2,1,0:T(1,128)S(1)} all-gather(f32[1,1,8192]{2,1,0:T(1,128)S(1)} %bitcast.1670), channel_id=1, replica_groups=mesh['gx_0'=4,'gx_1'=8,'gx_2'=2,'gy'=8] {'gx_0'}, dimensions={0}, use_global_device_ids=true | all-gather | bytes 163840 | tf_op jit(solution)/shard_map/all_gather | solution.py:30
  460.2 7.7 %subtract_bitcast_fusion.10 = (f32[1,1,8192]{2,1,0:T(1,128)S(1)}, f32[1,8192]{1,0:T(1,128)S(1)}, f32[1,8192]{1,0:T(1,128)S(1)}) fusion(f32[]{:T(128)S(6)} %div.116, f32[]{:T(128)} %bitcast.52, f32[]{:T(128)} %bitcast.54, f32[]{:T(128)} %bitcast.5, f32[1,8192]{1,0:T(1,128)S(1)} %bitcast.1705, f32[14,8192]{1,0:T(8,128)S(1)} %fusion.290, ...), kind=kLoop, calls=%fused_computation.679 | loop fusion | flops 401408 | bytes 688214
  470.4 24.8 %all-gather.26 = f32[8,1,8192]{2,1,0:T(1,128)S(1)} all-gather(f32[1,1,8192]{2,1,0:T(1,128)S(1)} %slice_add_fusion.32), channel_id=1, replica_groups=mesh['gx_0'=4,'gx_1'=8,'gx_2'=2,'gy'=8] {'gx_1'}, dimensions={0}, use_global_device_ids=true | all-gather | bytes 294912 | tf_op jit(solution)/shard_map/all_gather | solution.py:30
  499.7 12.0 %all-gather.27 = f32[4,1,8192]{2,1,0:T(1,128)S(1)} all-gather(f32[1,1,8192]{2,1,0:T(1,128)S(1)} %bitcast.1671), channel_id=1, replica_groups=mesh['gx_0'=4,'gx_1'=8,'gx_2'=2,'gy'=8] {'gx_0'}, dimensions={0}, use_global_device_ids=true | all-gather | bytes 163840 | tf_op jit(solution)/shard_map/all_gather | solution.py:30
  511.7 5.4 multiply_subtract_fusion.6
  522.5 24.8 %all-gather.29 = f32[8,1,8192]{2,1,0:T(1,128)S(1)} all-gather(f32[1,1,8192]{2,1,0:T(1,128)S(1)} %slice_add_fusion.24), channel_id=1, replica_groups=mesh['gx_0'=4,'gx_1'=8,'gx_2'=2,'gy'=8] {'gx_1'}, dimensions={0}, use_global_device_ids=true | all-gather | bytes 294912 | tf_op jit(solution)/shard_map/all_gather | solution.py:30
  547.3 4.5 fusion.143
  551.7 12.0 %all-gather.30 = f32[4,1,8192]{2,1,0:T(1,128)S(1)} all-gather(f32[1,1,8192]{2,1,0:T(1,128)S(1)} %bitcast.1672), channel_id=1, replica_groups=mesh['gx_0'=4,'gx_1'=8,'gx_2'=2,'gy'=8] {'gx_0'}, dimensions={0}, use_global_device_ids=true | all-gather | bytes 163840 | tf_op jit(solution)/shard_map/all_gather | solution.py:30
  563.7 7.7 %subtract_bitcast_fusion.8 = (f32[1,1,8192]{2,1,0:T(1,128)S(1)}, f32[1,8192]{1,0:T(1,128)S(1)}, f32[1,8192]{1,0:T(1,128)S(1)}) fusion(f32[]{:T(128)S(6)} %div.116, f32[]{:T(128)} %bitcast.52, f32[]{:T(128)} %bitcast.54, f32[]{:T(128)} %bitcast.5, f32[1,8192]{1,0:T(1,128)S(1)} %bitcast.1709, f32[14,8192]{1,0:T(8,128)S(1)} %fusion.291, ...), kind=kLoop, calls=%fused_computation.673 | loop fusion | flops 401408 | bytes 688214
  574.0 24.8 %all-gather.32 = f32[8,1,8192]{2,1,0:T(1,128)S(1)} all-gather(f32[1,1,8192]{2,1,0:T(1,128)S(1)} %slice_add_fusion.18), channel_id=1, replica_groups=mesh['gx_0'=4,'gx_1'=8,'gx_2'=2,'gy'=8] {'gx_1'}, dimensions={0}, use_global_device_ids=true | all-gather | bytes 294912 | tf_op jit(solution)/shard_map/all_gather | solution.py:30
  598.8 4.4 fusion.133
  603.2 12.0 %all-gather.33 = f32[4,1,8192]{2,1,0:T(1,128)S(1)} all-gather(f32[1,1,8192]{2,1,0:T(1,128)S(1)} %bitcast.1673), channel_id=1, replica_groups=mesh['gx_0'=4,'gx_1'=8,'gx_2'=2,'gy'=8] {'gx_0'}, dimensions={0}, use_global_device_ids=true | all-gather | bytes 163840 | tf_op jit(solution)/shard_map/all_gather | solution.py:30
  615.2 5.4 multiply_subtract_fusion.3
  626.0 24.8 %all-gather.35 = f32[8,1,8192]{2,1,0:T(1,128)S(1)} all-gather(f32[1,1,8192]{2,1,0:T(1,128)S(1)} %slice_add_fusion.10), channel_id=1, replica_groups=mesh['gx_0'=4,'gx_1'=8,'gx_2'=2,'gy'=8] {'gx_1'}, dimensions={0}, use_global_device_ids=true | all-gather | bytes 294912 | tf_op jit(solution)/shard_map/all_gather | solution.py:30
  650.8 4.5 fusion.119
  655.3 12.0 %all-gather.36 = f32[4,1,8192]{2,1,0:T(1,128)S(1)} all-gather(f32[1,1,8192]{2,1,0:T(1,128)S(1)} %bitcast.1664), channel_id=1, replica_groups=mesh['gx_0'=4,'gx_1'=8,'gx_2'=2,'gy'=8] {'gx_0'}, dimensions={0}, use_global_device_ids=true | all-gather | bytes 163840 | tf_op jit(solution)/shard_map/all_gather | solution.py:30
  667.3 7.7 %subtract_bitcast_fusion.6 = (f32[1,1,8192]{2,1,0:T(1,128)S(1)}, f32[1,8192]{1,0:T(1,128)S(1)}, f32[1,8192]{1,0:T(1,128)S(1)}) fusion(f32[]{:T(128)S(6)} %div.116, f32[]{:T(128)} %bitcast.52, f32[]{:T(128)} %bitcast.54, f32[]{:T(128)} %bitcast.5, f32[1,8192]{1,0:T(1,128)S(1)} %bitcast.1681, f32[14,8192]{1,0:T(8,128)S(1)} %fusion.292, ...), kind=kLoop, calls=%fused_computation.667 | loop fusion | flops 401408 | bytes 688214
  677.6 24.8 %all-gather.38 = f32[8,1,8192]{2,1,0:T(1,128)S(1)} all-gather(f32[1,1,8192]{2,1,0:T(1,128)S(1)} %slice_add_fusion.4), channel_id=1, replica_groups=mesh['gx_0'=4,'gx_1'=8,'gx_2'=2,'gy'=8] {'gx_1'}, dimensions={0}, use_global_device_ids=true | all-gather | bytes 294912 | tf_op jit(solution)/shard_map/all_gather | solution.py:30
  706.8 12.0 %all-gather.39 = f32[4,1,8192]{2,1,0:T(1,128)S(1)} all-gather(f32[1,1,8192]{2,1,0:T(1,128)S(1)} %bitcast.1665), channel_id=1, replica_groups=mesh['gx_0'=4,'gx_1'=8,'gx_2'=2,'gy'=8] {'gx_0'}, dimensions={0}, use_global_device_ids=true | all-gather | bytes 163840 | tf_op jit(solution)/shard_map/all_gather | solution.py:30
  718.8 5.4 multiply_subtract_fusion
  (203 shorter events, 116.4 us)
Async XLA Ops:
  0.0 1.6 copy-start.12
  0.0 2.3 copy-start.11
  0.0 2.9 copy-start.10
  0.0 43.2 %copy-start = (f32[3,16,16,512]{3,2,1,0:T(8,128)S(1)}, f32[3,16,16,512]{3,2,1,0:T(8,128)}, u32[]{:S(2)}) copy-start(f32[3,16,16,512]{3,2,1,0:T(8,128)} %param.46) | copy-start | bytes 4718596
  43.8 0.8 copy-start.3
  44.6 3.1 copy-start.5
  46.3 3.5 copy-start.6
  48.3 0.8 copy-start.1
  77.1 106.7 %copy-start.7 = (f32[14]{0:T(128)S(1)}, f32[14]{0:T(128)}, u32[]{:S(2)}) copy-start(f32[14]{0:T(128)} %constant.473) | copy-start | bytes 172
  77.1 106.7 %copy-start.8 = (f32[14]{0:T(128)S(1)}, f32[14]{0:T(128)}, u32[]{:S(2)}) copy-start(f32[14]{0:T(128)} %constant.476) | copy-start | bytes 172
  111.8 60.2 %copy-start.9 = (f32[4]{0:T(128)S(1)}, f32[4]{0:T(128)}, u32[]{:S(2)}) copy-start(f32[4]{0:T(128)} %get-tuple-element.225) | copy-start | bytes 52
  111.8 72.0 %copy-start.2 = (f32[14,8192]{1,0:T(8,128)S(1)}, f32[14,8192]{1,0:T(8,128)}, u32[]{:S(2)}) copy-start(f32[14,8192]{1,0:T(8,128)} %copy-done.1) | copy-start | bytes 1376260
  184.8 0.9 copy-start.4
  392.9 13.7 %collective-permute-start = (f32[3,16,1,512]{3,2,1,0:T(1,128)S(1)}, f32[3,16,1,512]{3,2,1,0:T(1,128)S(1)}, u32[]{:S(2)}, u32[]{:S(2)}) collective-permute-start(f32[3,16,1,512]{3,2,1,0:T(1,128)S(1)} %get-tuple-element.312), channel_id=1, source_target_pairs={{1,0},{2,1},{3,2},{4,3},{5,4},{6,5},{7,6},{0,7},{9,8},{10,9},{11,1... | collective-permute-start | bytes 294920 | tf_op jit(solution)/shard_map/ppermute | solution.py:49
  403.5 7.7 %collective-permute-start.1 = (f32[3,16,1,512]{3,2,1,0:T(1,128)S(1)}, f32[3,16,1,512]{3,2,1,0:T(1,128)S(1)}, u32[]{:S(2)}, u32[]{:S(2)}) collective-permute-start(f32[3,16,1,512]{3,2,1,0:T(1,128)S(1)} %get-tuple-element.313), channel_id=1, source_target_pairs={{0,1},{1,2},{2,3},{3,4},{4,5},{5,6},{6,7},{7,0},{8,9},{9,10},{10,1... | collective-permute-start | bytes 294920 | tf_op jit(solution)/shard_map/ppermute | solution.py:46
  725.8 6.5 collective-permute-start.2
  727.7 7.7 %collective-permute-start.3 = (f32[3,16,1,512]{3,2,1,0:T(1,128)S(1)}, f32[3,16,1,512]{3,2,1,0:T(1,128)S(1)}, u32[]{:S(2)}, u32[]{:S(2)}) collective-permute-start(f32[3,16,1,512]{3,2,1,0:T(1,128)S(1)} %get-tuple-element.307), channel_id=1, source_target_pairs={{0,1},{1,2},{2,3},{3,4},{4,5},{5,6},{6,7},{7,0},{8,9},{9,10},{10,1... | collective-permute-start | bytes 294920 | tf_op jit(solution)/shard_map/ppermute | solution.py:46
where the time goes:
time: 750 us; the launch traced here: 740 us
  blocking collectives  495 us (66%)
  other arithmetic  163 us (22%)
  local copies, waits for them, and re-layouts  30.6 us (4%)
  between operations  21.7 us (3%)
  starting transfers between devices  18.6 us (2%)
  waiting for transfers between devices  7.76 us (1%)
    all_gather x36, blocking collectives, entering(): pieces = jax.tree.map(lambda part: lax.all_gather(part, axis), total)  466 us
    add x24, other arithmetic, compose(): return (earlier[0] * later[0], later[0] * earlier[1] + later[1])  61.6 us
    unnamed x18, other arithmetic  52.6 us
    sub x6, other arithmetic, per_device(): first_value = scaled_first - ratio_first * last_value  32.4 us
    unnamed x3, blocking collectives  28.6 us
    unnamed x84, local copies, waits for them, and re-layouts  23.3 us
  transfers between devices with their start and end apart: 4, of which 2 were waited for; matrix products, arithmetic and copies ran while one was open for 0% of the time, Pallas kernels for 0%

commit v1 on v0

v1 whole, which is shorter than its diff:
```python
import functools
import math

import jax
import jax.numpy as jnp
from jax import lax
from jax.experimental import pallas as pl
from jax.experimental.pallas import tpu as pltpu
from jax.sharding import PartitionSpec as P

STEPS = 2
MESH = pl.DeviceIdType.MESH
LANES = 128
ROWS = 8
COEFS = 16
WAVES = 8

diffusion = 4000.0
anisotropy_rate = 0.3
torque_rate = 0.2
exchange_rate = 0.1
norm_floor = 0.5

half_trace = (1.0 + 2.0 * diffusion) / (2.0 * diffusion)
decay = half_trace - math.sqrt(half_trace * half_trace - 1.0)
weight = 1.0 / (diffusion * (1.0 / decay - decay))


def sweep(count, carry, body, reverse=False, unroll=8):
    def chunk(step, carry):
        base = pl.multiple_of((count // unroll - 1 - step if reverse else step) * unroll, unroll)
        for k in reversed(range(unroll)) if reverse else range(unroll):
            carry = body(base, k, carry)
        return carry

    return lax.fori_loop(0, count // unroll, chunk, carry)


def wave_maps(thick, lanes, m, a, tp, ts, tq, tk, put, with_coefs):
    zero = jnp.zeros((ROWS, LANES), jnp.float32)
    r2 = decay * decay
    rate = anisotropy_rate

    def load(ref, i):
        return tuple(ref[c, i, :, lanes] for c in range(3))

    def up1(base, k, p):
        i = base + k
        m1, m2, m3 = load(m, i)
        a1, a2, a3 = load(a, i)
        cs = weight * (m1 + rate * a1 * (a1 * m1 + a2 * m2 + a3 * m3))
        p = decay * p + cs
        tp[i] = p
        ts[i] = cs
        return p

    put(0, sweep(thick, zero, up1))

    def down(base, k, carry):
        i = base + k
        qs, qs2, qk, g23, sum12 = carry
        m1, m2, m3 = load(m, i)
        a1, a2, a3 = load(a, i)
        q = decay * qs
        f1 = tp[i] + q
        qs = q + ts[i]
        cs2 = weight * (m2 + rate * a2 * (a1 * f1 + a2 * m2 + a3 * m3))
        q2 = decay * qs2
        qs2 = q2 + cs2
        tp[i] = f1
        ts[i] = cs2
        tq[i] = q2
        if with_coefs:
            k12 = (weight * decay * rate) * a1 * a2
            down_k = r2 * qk
            tk[i] = down_k
            qk = down_k + k12
            sum12 = sum12 + k12
            g23 = r2 * g23 + (weight * decay * rate) * a2 * a3
        return qs, qs2, qk, g23, sum12

    r1_out, r2_out, alpha12, alpha23, sum12 = sweep(thick, (zero,) * 5, down, reverse=True)
    put(1, r1_out)
    put(3, r2_out)

    def up2(base, k, carry):
        i = base + k
        p2, l3, r3, w, pk, sk, h23, sum23, l3p, l3s, r3p, r3s = carry
        m3 = m[2, i, :, lanes]
        a1, a2, a3 = load(a, i)
        p2 = decay * p2 + ts[i]
        f2 = p2 + tq[i]
        cs3 = weight * (m3 + rate * a3 * (a1 * tp[i] + a2 * f2 + a3 * m3))
        l3 = decay * l3 + cs3
        r3 = r3 + w * cs3
        if with_coefs:
            k12 = (weight * decay * rate) * a1 * a2
            k13 = (weight * decay * rate) * a1 * a3
            k23 = (weight * rate) * a2 * a3
            pk = pk + k12
            sk = r2 * sk + k12
            tau_p = k13 + k23 * (pk + tk[i])
            tau_s = k13 + k23 * (sk + (sum12 - pk))
            h23 = r2 * h23 + k23
            sum23 = sum23 + k23
            l3p = l3p + tau_p
            r3p = r3p + (w * w) * tau_p
            l3s = r2 * l3s + tau_s
            r3s = r3s + tau_s
        w = w * decay
        return p2, l3, r3, w, pk, sk, h23, sum23, l3p, l3s, r3p, r3s

    one = jnp.ones((ROWS, LANES), jnp.float32)
    p2, l3, r3, _, _, gamma12, h23, sum23, l3p, l3s, r3p, r3s = sweep(
        thick, (zero, zero, zero, one) + (zero,) * 8, up2, unroll=4
    )
    put(2, p2)
    put(4, l3)
    put(5, r3)
    if with_coefs:
        across = decay ** (thick - 1)
        put(6, alpha12)
        put(7, across * sum12)
        put(8, gamma12)
        put(9, alpha23)
        put(10, (across * decay) * sum23)
        put(11, decay * h23)
        put(12, across * l3p)
        put(13, l3s)
        put(14, r3p)
        put(15, across * r3s)


def solved_fields(thick, lanes, m, a, f, tp, ts, tq, get, edge):
    rate = anisotropy_rate

    def load(ref, i):
        return tuple(ref[c, i, :, lanes] for c in range(3))

    def keep(c, base, k, value):
        f[c, base + k, :, lanes] = value
        edge.at[0, c, pl.ds(base, 8), lanes][k : k + 1] = value[0:1]
        edge.at[1, c, pl.ds(base, 8), lanes][k : k + 1] = value[ROWS - 1 : ROWS]

    def up1(base, k, p):
        i = base + k
        m1, m2, m3 = load(m, i)
        a1, a2, a3 = load(a, i)
        cs = weight * (m1 + rate * a1 * (a1 * m1 + a2 * m2 + a3 * m3))
        p = decay * p + cs
        tp[i] = p
        ts[i] = cs
        return p

    sweep(thick, get(0), up1)

    def down(base, k, carry):
        i = base + k
        qs, qs2 = carry
        _, m2, m3 = load(m, i)
        a1, a2, a3 = load(a, i)
        q = decay * qs
        f1 = tp[i] + q
        qs = q + ts[i]
        keep(0, base, k, f1)
        cs2 = weight * (m2 + rate * a2 * (a1 * f1 + a2 * m2 + a3 * m3))
        q2 = decay * qs2
        qs2 = q2 + cs2
        ts[i] = cs2
        tq[i] = q2
        return qs, qs2

    sweep(thick, (get(1), get(3)), down, reverse=True)

    def up2(base, k, carry):
        i = base + k
        p2, p3 = carry
        m3 = m[2, i, :, lanes]
        a1, a2, a3 = load(a, i)
        p2 = decay * p2 + ts[i]
        f2 = p2 + tq[i]
        keep(1, base, k, f2)
        cs3 = weight * (m3 + rate * a3 * (a1 * f[0, i, :, lanes] + a2 * f2 + a3 * m3))
        p3 = decay * p3 + cs3
        tp[i] = p3
        ts[i] = cs3
        return p2, p3

    sweep(thick, (get(2), get(4)), up2)

    def down2(base, k, qs):
        i = base + k
        q = decay * qs
        keep(2, base, k, tp[i] + q)
        return q + ts[i]

    sweep(thick, get(5), down2, reverse=True)


def owner_solve(chips, thick, value, coef, pin, put):
    depth = chips // ROWS
    hop = decay**thick
    sub = lax.broadcasted_iota(jnp.int32, (ROWS, LANES), 0)

    def powers(number):
        out = jnp.ones((ROWS, LANES), jnp.float32)
        for bit in (1, 2, 4):
            out = out * jnp.where((number // bit) % 2 == 1, hop ** (depth * bit), 1.0)
        return out

    rising, falling = powers(sub), powers(ROWS - 1 - sub)

    def scan_up(x):
        inside = [jnp.zeros((ROWS, LANES), jnp.float32)]
        for t in range(depth):
            inside.append(hop * inside[-1] + x[t])
        total = inside.pop()
        for shift in (1, 2, 4):
            moved = jnp.where(sub >= shift, pltpu.roll(total, shift, 0), 0.0)
            total = total + hop ** (depth * shift) * moved
        before = jnp.where(sub >= 1, pltpu.roll(total, 1, 0), 0.0)
        return [inside[t] + hop**t * before for t in range(depth)], total[ROWS - 1 : ROWS]

    def scan_down(x):
        inside = [jnp.zeros((ROWS, LANES), jnp.float32)]
        for t in reversed(range(depth)):
            inside.append(hop * inside[-1] + x[t])
        total = inside.pop()
        inside = inside[::-1]
        for shift in (1, 2, 4):
            moved = jnp.where(sub < ROWS - shift, pltpu.roll(total, ROWS - shift, 0), 0.0)
            total = total + hop ** (depth * shift) * moved
        before = jnp.where(sub < ROWS - 1, pltpu.roll(total, ROWS - 1, 0), 0.0)
        return [inside[t] + hop ** (depth - 1 - t) * before for t in range(depth)], total[0:1]

    end = decay * hop**chips

    def line(left, right, component):
        up, up_end = scan_up(left)
        down, down_end = scan_down(right)
        first = pin(0, component) - decay * down_end
        last = pin(1, component) - decay * up_end
        alpha = (first - end * last) * (1.0 / (1.0 - end * end))
        beta = (last - end * first) * (1.0 / (1.0 - end * end))
        up = [up[t] + (hop**t * rising) * alpha for t in range(depth)]
        down = [down[t] + (hop ** (depth - 1 - t) * falling) * beta for t in range(depth)]
        for t in range(depth):
            put(2 * component, t, up[t])
            put(2 * component + 1, t, down[t])
        return up, down

    span = range(depth)
    p1, s1 = line([value(0, t) for t in span], [value(1, t) for t in span], 0)
    p2, s2 = line(
        [value(2, t) + coef(7, t) * p1[t] + coef(8, t) * s1[t] for t in span],
        [value(3, t) + coef(6, t) * p1[t] + coef(7, t) * s1[t] for t in span],
        1,
    )
    line(
        [
            value(4, t) + coef(12, t) * p1[t] + coef(13, t) * s1[t] + coef(10, t) * p2[t] + coef(11, t) * s2[t]
            for t in span
        ],
        [
            value(5, t) + coef(14, t) * p1[t] + coef(15, t) * s1[t] + coef(9, t) * p2[t] + coef(10, t) * s2[t]
            for t in span
        ],
        2,
    )


def torque(planes_from, planes, f, a, halo, out):
    wide = f.shape[-1]
    sub = lax.broadcasted_iota(jnp.int32, (ROWS, wide), 0)

    def chunk(step, carry):
        base = pl.multiple_of(planes_from + step * 8, 8)
        for k in range(8):
            plane(base, k)
        return carry

    def plane(base, k):
        i = base + k
        field = [f[c, i] for c in range(3)]
        axes = [a[c, i] for c in range(3)]
        projection = field[0] * axes[0] + field[1] * axes[1] + field[2] * axes[2]
        effective = []
        for c in range(3):
            low = jnp.where(sub == 0, halo[0, c, pl.ds(base, 8)][k : k + 1], pltpu.roll(field[c], 1, 0))
            high = jnp.where(sub == ROWS - 1, halo[1, c, pl.ds(base, 8)][k : k + 1], pltpu.roll(field[c], ROWS - 1, 0))
            sides = low + high + pltpu.roll(field[c], 1, 1) + pltpu.roll(field[c], wide - 1, 1)
            effective.append(exchange_rate * (sides - 4.0 * field[c]) + projection * axes[c])
        rotated = []
        for c in range(3):
            b, d = (c + 1) % 3, (c + 2) % 3
            rotated.append(field[c] - torque_rate * (field[b] * effective[d] - field[d] * effective[b]))
        square = rotated[0] * rotated[0] + rotated[1] * rotated[1] + rotated[2] * rotated[2]
        scale = lax.rsqrt(jnp.maximum(square, norm_floor * norm_floor))
        for c in range(3):
            out[c, i] = rotated[c] * scale

    lax.fori_loop(0, planes // 8, chunk, 0)


def kernel(
    chips, ring, groups,
    m_hbm, a_hbm, pins_hbm, out_hbm,
    m, a, f, pins, tp, ts, tq, tk, send1, got1, send2, got2, back, waves, edge, halo,
    load_sem, swap_send, swap_recv, send_sem, recv_sem, edge_send, edge_recv, out_sem, out_send, out_recv,
):
    position, group = lax.axis_index("gx"), lax.axis_index("gy")
    chip, core = position // 2, position % 2
    other = 1 - core
    partner = chip * 2 + other
    half = m_hbm.shape[1]
    thick = 2 * half
    tiles = m.shape[-1] // LANES
    low = (partner, (group + groups - other) % groups)
    high = (partner, (group + core) % groups)
    mine_rows = pl.ds(pl.multiple_of(core * ROWS, ROWS), ROWS)
    other_rows = pl.ds(pl.multiple_of(other * ROWS, ROWS), ROWS)
    mine_planes = pl.ds(core * half, half)
    other_planes = pl.ds(other * half, half)

    loads = [
        pltpu.make_async_copy(a_hbm.at[:, :, mine_rows], a.at[:, mine_planes], load_sem.at[0]),
        pltpu.make_async_copy(m_hbm.at[:, :, mine_rows], m.at[:, mine_planes], load_sem.at[1]),
        pltpu.make_async_copy(pins_hbm.at[:, :, mine_rows], pins, load_sem.at[2]),
    ]

    columns = chips // ring

    def zigzag(k):
        return ((k + 1) // 2) * (2 * ((k + 1) % 2) - 1)

    def peer(t):
        dx = columns // 2 + zigzag(t % columns)
        dy = ring // 2 + zigzag(t // columns)
        return ((chip // ring + dx) % columns) * ring + (chip % ring + dy) % ring

    barrier = pltpu.get_barrier_semaphore()

    def greet(t, carry):
        pl.semaphore_signal(barrier, inc=1, device_id=(peer(t) * 2 + core, group), device_id_type=MESH)
        return carry

    lax.fori_loop(0, chips - 1, greet, 0)
    for neighbour in (low, high):
        pl.semaphore_signal(barrier, inc=1, device_id=neighbour, device_id_type=MESH)
    for copy in loads:
        copy.start()
    pl.semaphore_wait(barrier, chips + 1)

    swaps = [
        pltpu.make_async_remote_copy(
            src_ref=hbm.at[:, :, other_rows],
            dst_ref=vmem.at[:, mine_planes],
            send_sem=swap_send.at[k],
            recv_sem=swap_recv.at[k],
            device_id=(partner, group),
            device_id_type=MESH,
        )
        for k, (hbm, vmem) in enumerate(((a_hbm, a), (m_hbm, m)))
    ]
    for copy in swaps:
        copy.start()
    for copy in loads + swaps:
        copy.wait()

    def exchange(phase, source, target, stride, size):
        def start(t, carry):
            to = peer(t)
            pltpu.make_async_remote_copy(
                src_ref=source.at[pl.ds(pl.multiple_of(to * stride, 8), size)],
                dst_ref=target.at[pl.ds(pl.multiple_of(chip * stride, 8), size)],
                send_sem=send_sem.at[phase],
                recv_sem=recv_sem.at[phase],
                device_id=(to * 2 + core, group),
                device_id_type=MESH,
            ).start()
            return carry

        lax.fori_loop(0, chips - 1, start, 0)
        own = pl.ds(pl.multiple_of(chip * stride, 8), size)
        target[own] = source[own]
        total = pl.ds(0, (chips - 1) * size)
        pltpu.make_async_remote_copy(
            src_ref=source.at[total],
            dst_ref=target.at[total],
            send_sem=send_sem.at[phase],
            recv_sem=recv_sem.at[phase],
            device_id=(partner, group),
            device_id_type=MESH,
        ).wait()

    depth = chips // ROWS
    for step in range(STEPS):
        source, target, stride = (send1, got1, COEFS) if step == 0 else (send2, got2, WAVES)

        def maps_tile(tile, carry):
            lanes = pl.ds(pl.multiple_of(tile * LANES, LANES), LANES)

            def put(v, value):
                source[pl.ds(tile * (ROWS * stride) + v, ROWS, stride=stride), :] = value

            wave_maps(thick, lanes, m, a, tp, ts, tq, tk, put, step == 0)
            return carry

        lax.fori_loop(0, tiles, maps_tile, 0)
        exchange(2 * step, source, target, stride, stride)

        def value(v, t):
            return target[pl.ds(t * stride + v, ROWS, stride=depth * stride), :]

        def coef(v, t):
            return got1[pl.ds(t * COEFS + v, ROWS, stride=depth * COEFS), :]

        def pin(side, component):
            lanes = pl.ds(pl.multiple_of((chip // ROWS) * LANES, LANES), LANES)
            sub = lax.broadcasted_iota(jnp.int32, (ROWS, LANES), 0)
            return jnp.sum(jnp.where(sub == chip % ROWS, pins[side, component, :, lanes], 0.0), axis=0, keepdims=True)

        def put_wave(v, t, value):
            back[pl.ds(t * WAVES + v, ROWS, stride=depth * WAVES), :] = value

        owner_solve(chips, thick, value, coef, pin, put_wave)
        wave = waves.at[step]
        exchange(2 * step + 1, back, wave, WAVES, WAVES)

        def solve_tile(tile, carry):
            lanes = pl.ds(pl.multiple_of(tile * LANES, LANES), LANES)

            def get(v):
                return wave[pl.ds(tile * (ROWS * WAVES) + v, ROWS, stride=WAVES), :]

            solved_fields(thick, lanes, m, a, f, tp, ts, tq, get, edge)
            return carry

        lax.fori_loop(0, tiles, solve_tile, 0)
        borders = [
            pltpu.make_async_remote_copy(
                src_ref=edge.at[k],
                dst_ref=halo.at[step, 1 - k],
                send_sem=edge_send.at[2 * step + k],
                recv_sem=edge_recv.at[2 * step + k],
                device_id=neighbour,
                device_id_type=MESH,
            )
            for k, neighbour in enumerate((low, high))
        ]
        for copy in borders:
            copy.start()
        for copy in borders:
            copy.wait()
        if step < STEPS - 1:
            torque(0, thick, f, a, halo.at[step], m)

    out_far = pltpu.make_async_remote_copy(
        src_ref=m.at[:, other_planes],
        dst_ref=out_hbm.at[:, :, mine_rows],
        send_sem=out_send,
        recv_sem=out_recv,
        device_id=(partner, group),
        device_id_type=MESH,
    )
    out_here = pltpu.make_async_copy(m.at[:, mine_planes], out_hbm.at[:, :, mine_rows], out_sem)
    torque(other * half, half, f, a, halo.at[STEPS - 1], m)
    out_far.start()
    torque(core * half, half, f, a, halo.at[STEPS - 1], m)
    out_here.start()
    out_here.wait()
    out_far.wait()


def per_device(chips, ring, groups, magnetization, easy_axes, pins):
    _, half, rows, wide = magnetization.shape
    thick = 2 * half
    blocks = chips * WAVES
    f32 = jnp.float32
    any_space = pl.BlockSpec(memory_space=pl.ANY)
    dma = pltpu.SemaphoreType.DMA
    return pl.pallas_call(
        functools.partial(kernel, chips, ring, groups),
        out_shape=jax.ShapeDtypeStruct(magnetization.shape, f32),
        in_specs=[any_space] * 3,
        out_specs=any_space,
        scratch_shapes=[
            pltpu.VMEM((3, thick, ROWS, wide), f32),
            pltpu.VMEM((3, thick, ROWS, wide), f32),
            pltpu.VMEM((3, thick, ROWS, wide), f32),
            pltpu.VMEM((2, 3, ROWS, wide), f32),
            pltpu.VMEM((thick, ROWS, LANES), f32),
            pltpu.VMEM((thick, ROWS, LANES), f32),
            pltpu.VMEM((thick, ROWS, LANES), f32),
            pltpu.VMEM((thick, ROWS, LANES), f32),
            pltpu.VMEM((chips * COEFS, LANES), f32),
            pltpu.VMEM((chips * COEFS, LANES), f32),
            pltpu.VMEM((blocks, LANES), f32),
            pltpu.VMEM((blocks, LANES), f32),
            pltpu.VMEM((blocks, LANES), f32),
            pltpu.VMEM((STEPS, blocks, LANES), f32),
            pltpu.VMEM((2, 3, thick, wide), f32),
            pltpu.VMEM((STEPS, 2, 3, thick, wide), f32),
            dma((3,)),
            dma((2,)),
            dma((2,)),
            dma((2 * STEPS,)),
            dma((2 * STEPS,)),
            dma((2 * STEPS,)),
            dma((2 * STEPS,)),
            dma,
            dma,
            dma,
        ],
        compiler_params=pltpu.CompilerParams(collective_id=0, has_side_effects=True),
    )(magnetization, easy_axes, pins)


def solution(mesh):
    chips, groups = mesh.shape["gx"] // 2, mesh.shape["gy"]
    body = functools.partial(per_device, chips, 8 if chips % 8 == 0 else 1, groups)
    spec = P(None, "gx", "gy", None)
    return jax.shard_map(
        body, mesh=mesh, in_specs=(spec, spec, P(None, None, "gy", None)), out_specs=spec, check_vma=False
    )
```

time: 750 us -> 71.3 us (0.10)
  the two profiles are of different devices: /device:TPU:4 before, /device:TPU:1 now
where the time goes in v1:
time: 71.3 us; the launch traced here: 71.1 us
  Pallas kernels  68.3 us (96%)
  local copies, waits for them, and re-layouts  2.77 us (4%)
    pallas_call x1, Pallas kernels, per_device(): pl.pallas_call(functools.partial(kernel, chips, ring, groups), out_shape=...  68.3 us
    unnamed x1, local copies, waits for them, and re-layouts  2.77 us

profile of v1, /device:TPU:1, one launch (start us, length us, event | category | flops | bytes accessed | tf_op | source)
XLA Modules:
  0.0 71.1 jit_solution(632899332909344722)
XLA Ops:
  0.0 68.3 %shard_map.37 = f32[3,16,16,512]{3,2,1,0:T(8,128)} custom-call(f32[3,16,16,512]{3,2,1,0:T(8,128)} %m_hbm.1, f32[3,16,16,512]{3,2,1,0:T(8,128)} %a_hbm.1, f32[2,3,16,512]{3,2,1,0:T(8,128)} %pins_hbm.1), custom_call_target="tpu_custom_call" | custom-call | tf_op jit(solution)/shard_map/pallas_call | solution.py:482
  68.3 2.8 %copy.5 = f32[3,16,16,512]{3,2,1,0:T(8,128)} copy(f32[3,16,16,512]{3,2,1,0:T(8,128)} %shard_map.37) | data formatting | bytes 3145728

commit v2 on v1

--- a/solution.py
+++ b/solution.py
@@ -131,7 +131,7 @@
         put(15, across * r3s)
 
 
-def solved_fields(thick, lanes, m, a, f, tp, ts, tq, get, edge):
+def solved_fields(thick, lanes, m, a, f, tp, ts, tq, get, first, last):
     rate = anisotropy_rate
 
     def load(ref, i):
@@ -139,8 +139,8 @@
 
     def keep(c, base, k, value):
         f[c, base + k, :, lanes] = value
-        edge.at[0, c, pl.ds(base, 8), lanes][k : k + 1] = value[0:1]
-        edge.at[1, c, pl.ds(base, 8), lanes][k : k + 1] = value[ROWS - 1 : ROWS]
+        first.at[c, pl.ds(base, 8)][k : k + 1] = value[0:1]
+        last.at[c, pl.ds(base, 8)][k : k + 1] = value[ROWS - 1 : ROWS]
 
     def up1(base, k, p):
         i = base + k
@@ -275,19 +275,22 @@
 
     def chunk(step, carry):
         base = pl.multiple_of(planes_from + step * 8, 8)
+        rows = [
+            [jnp.concatenate([halo[side, t, c, pl.ds(base, 8)] for t in range(wide // LANES)], axis=1) for c in range(3)]
+            for side in range(2)
+        ]
         for k in range(8):
-            plane(base, k)
+            plane(base + k, k, rows)
         return carry
 
-    def plane(base, k):
-        i = base + k
+    def plane(i, k, rows):
         field = [f[c, i] for c in range(3)]
         axes = [a[c, i] for c in range(3)]
         projection = field[0] * axes[0] + field[1] * axes[1] + field[2] * axes[2]
         effective = []
         for c in range(3):
-            low = jnp.where(sub == 0, halo[0, c, pl.ds(base, 8)][k : k + 1], pltpu.roll(field[c], 1, 0))
-            high = jnp.where(sub == ROWS - 1, halo[1, c, pl.ds(base, 8)][k : k + 1], pltpu.roll(field[c], ROWS - 1, 0))
+            low = jnp.where(sub == 0, rows[0][c][k : k + 1], pltpu.roll(field[c], 1, 0))
+            high = jnp.where(sub == ROWS - 1, rows[1][c][k : k + 1], pltpu.roll(field[c], ROWS - 1, 0))
             sides = low + high + pltpu.roll(field[c], 1, 1) + pltpu.roll(field[c], wide - 1, 1)
             effective.append(exchange_rate * (sides - 4.0 * field[c]) + projection * axes[c])
         rotated = []
@@ -306,7 +309,7 @@
     chips, ring, groups,
     m_hbm, a_hbm, pins_hbm, out_hbm,
     m, a, f, pins, tp, ts, tq, tk, send1, got1, send2, got2, back, waves, edge, halo,
-    load_sem, swap_send, swap_recv, send_sem, recv_sem, edge_send, edge_recv, out_sem, out_send, out_recv,
+    load_sem, swap_send, swap_recv, map_send, map_recv, wave_send, wave_recv, edge_send, edge_recv, out_sem, out_send, out_recv,
 ):
     position, group = lax.axis_index("gx"), lax.axis_index("gy")
     chip, core = position // 2, position % 2
@@ -315,6 +318,7 @@
     half = m_hbm.shape[1]
     thick = 2 * half
     tiles = m.shape[-1] // LANES
+    here = chip // ring
     low = (partner, (group + groups - other) % groups)
     high = (partner, (group + core) % groups)
     mine_rows = pl.ds(pl.multiple_of(core * ROWS, ROWS), ROWS)
@@ -328,15 +332,20 @@
         pltpu.make_async_copy(pins_hbm.at[:, :, mine_rows], pins, load_sem.at[2]),
     ]
 
-    columns = chips // ring
-
     def zigzag(k):
         return ((k + 1) // 2) * (2 * ((k + 1) % 2) - 1)
 
+    def far_tile(j):
+        return (here + tiles // 2 + zigzag(j)) % tiles
+
+    def far_chip(tile, k):
+        return tile * ring + (chip % ring + ring // 2 + zigzag(k)) % ring
+
     def peer(t):
-        dx = columns // 2 + zigzag(t % columns)
-        dy = ring // 2 + zigzag(t // columns)
-        return ((chip // ring + dx) % columns) * ring + (chip % ring + dy) % ring
+        return far_chip(far_tile(t % tiles), t // tiles)
+
+    def lanes_of(tile):
+        return pl.ds(pl.multiple_of(tile * LANES, LANES), LANES)
 
     barrier = pltpu.get_barrier_semaphore()
 
@@ -351,138 +360,166 @@
         copy.start()
     pl.semaphore_wait(barrier, chips + 1)
 
-    swaps = [
-        pltpu.make_async_remote_copy(
-            src_ref=hbm.at[:, :, other_rows],
-            dst_ref=vmem.at[:, mine_planes],
-            send_sem=swap_send.at[k],
-            recv_sem=swap_recv.at[k],
+    def swaps(j):
+        lanes = lanes_of(far_tile(j))
+        return [
+            pltpu.make_async_remote_copy(
+                src_ref=hbm.at[:, :, other_rows, lanes],
+                dst_ref=vmem.at[:, mine_planes, :, lanes],
+                send_sem=swap_send.at[2 * j + k],
+                recv_sem=swap_recv.at[2 * j + k],
+                device_id=(partner, group),
+                device_id_type=MESH,
+            )
+            for k, (hbm, vmem) in enumerate(((a_hbm, a), (m_hbm, m)))
+        ]
+
+    def start_swap(j, carry):
+        for copy in swaps(j):
+            copy.start()
+        return carry
+
+    lax.fori_loop(0, tiles, start_swap, 0)
+    for copy in loads:
+        copy.wait()
+
+    depth = chips // ROWS
+    for step in range(STEPS):
+        source, target, stride = (send1, got1, COEFS) if step == 0 else (send2, got2, WAVES)
+
+        def block(number, stride):
+            return pl.ds(pl.multiple_of(number * stride, 8), stride)
+
+        def message(source, target, stride, to, sends, recvs):
+            return pltpu.make_async_remote_copy(
+                src_ref=source.at[block(to, stride)],
+                dst_ref=target.at[block(chip, stride)],
+                send_sem=sends,
+                recv_sem=recvs,
+                device_id=(to * 2 + core, group),
+                device_id_type=MESH,
+            )
+
+        def own_message(source, target, stride, recvs):
+            return pltpu.make_async_copy(source.at[block(chip, stride)], target.at[block(chip, stride)], recvs)
+
+        def maps_tile(j, carry):
+            tile = far_tile(j)
+            if step == 0:
+                for copy in swaps(j):
+                    copy.wait()
+
+            def put(v, value):
+                source[pl.ds(tile * (ROWS * stride) + v, ROWS, stride=stride), :] = value
+
+            wave_maps(thick, lanes_of(tile), m, a, tp, ts, tq, tk, put, step == 0)
+
+            def start(k, carry):
+                message(source, target, stride, far_chip(tile, k), map_send.at[step], map_recv.at[step]).start()
+                return carry
+
+            return lax.fori_loop(0, ring - (j + 1) // tiles, start, carry)
+
+        lax.fori_loop(0, tiles, maps_tile, 0)
+        own_message(source, target, stride, map_recv.at[step]).start()
+        pltpu.make_async_copy(source, target, map_recv.at[step]).wait()
+
+        def value(v, t):
+            return target[pl.ds(t * stride + v, ROWS, stride=depth * stride), :]
+
+        def coef(v, t):
+            return got1[pl.ds(t * COEFS + v, ROWS, stride=depth * COEFS), :]
+
+        def pin(side, component):
+            sub = lax.broadcasted_iota(jnp.int32, (ROWS, LANES), 0)
+            row = pins[side, component, :, lanes_of(here)]
+            return jnp.sum(jnp.where(sub == chip % ROWS, row, 0.0), axis=0, keepdims=True)
+
+        out_waves, wave = back.at[step], waves.at[step]
+
+        def put_wave(v, t, value):
+            out_waves[pl.ds(t * WAVES + v, ROWS, stride=depth * WAVES), :] = value
+
+        owner_solve(chips, thick, value, coef, pin, put_wave)
+
+        def send_wave(t, carry):
+            message(out_waves, wave, WAVES, peer(t), wave_send.at[step], wave_recv.at[step * tiles + here]).start()
+            return carry
+
+        lax.fori_loop(0, chips - 1, send_wave, 0)
+        own_message(out_waves, wave, WAVES, wave_recv.at[step * tiles + here]).start()
+
+        def border(side, tile):
+            return pltpu.make_async_remote_copy(
+                src_ref=edge.at[step, side, tile],
+                dst_ref=halo.at[step, 1 - side, tile],
+                send_sem=edge_send.at[2 * step + side],
+                recv_sem=edge_recv.at[2 * step + 1 - side],
+                device_id=(low, high)[side],
+                device_id_type=MESH,
+            )
+
+        def solve_tile(j, carry):
+            tile = far_tile(tiles - 1 - j)
+            rows = pl.ds(pl.multiple_of(tile * (ring * WAVES), 8), ring * WAVES)
+            pltpu.make_async_copy(out_waves.at[rows], wave.at[rows], wave_recv.at[step * tiles + tile]).wait()
+
+            def get(v):
+                return wave[pl.ds(tile * (ROWS * WAVES) + v, ROWS, stride=WAVES), :]
+
+            solved_fields(thick, lanes_of(tile), m, a, f, tp, ts, tq, get, edge.at[step, 0, tile], edge.at[step, 1, tile])
+            for side in range(2):
+                border(side, tile).start()
+            return carry
+
+        lax.fori_loop(0, tiles, solve_tile, 0)
+        for side in range(2):
+            pltpu.make_async_copy(edge.at[step, side], halo.at[step, side], edge_recv.at[2 * step + side]).wait()
+        if step < STEPS - 1:
+            torque(0, thick, f, a, halo.at[step], m)
+
+    def far_part(part):
+        planes = pl.ds(other * half + part * 8, 8)
+        return pltpu.make_async_remote_copy(
+            src_ref=m.at[:, planes],
+            dst_ref=out_hbm.at[:, pl.ds(part * 8, 8), mine_rows],
+            send_sem=out_send.at[part],
+            recv_sem=out_recv.at[part],
             device_id=(partner, group),
             device_id_type=MESH,
         )
-        for k, (hbm, vmem) in enumerate(((a_hbm, a), (m_hbm, m)))
-    ]
-    for copy in swaps:
-        copy.start()
-    for copy in loads + swaps:
-        copy.wait()
-
-    def exchange(phase, source, target, stride, size):
-        def start(t, carry):
-            to = peer(t)
-            pltpu.make_async_remote_copy(
-                src_ref=source.at[pl.ds(pl.multiple_of(to * stride, 8), size)],
-                dst_ref=target.at[pl.ds(pl.multiple_of(chip * stride, 8), size)],
-                send_sem=send_sem.at[phase],
-                recv_sem=recv_sem.at[phase],
-                device_id=(to * 2 + core, group),
-                device_id_type=MESH,
-            ).start()
-            return carry
-
-        lax.fori_loop(0, chips - 1, start, 0)
-        own = pl.ds(pl.multiple_of(chip * stride, 8), size)
-        target[own] = source[own]
-        total = pl.ds(0, (chips - 1) * size)
-        pltpu.make_async_remote_copy(
-            src_ref=source.at[total],
-            dst_ref=target.at[total],
-            send_sem=send_sem.at[phase],
-            recv_sem=recv_sem.at[phase],
-            device_id=(partner, group),
-            device_id_type=MESH,
-        ).wait()
-
-    depth = chips // ROWS
-    for step in range(STEPS):
-        source, target, stride = (send1, got1, COEFS) if step == 0 else (send2, got2, WAVES)
-
-        def maps_tile(tile, carry):
-            lanes = pl.ds(pl.multiple_of(tile * LANES, LANES), LANES)
-
-            def put(v, value):
-                source[pl.ds(tile * (ROWS * stride) + v, ROWS, stride=stride), :] = value
-
-            wave_maps(thick, lanes, m, a, tp, ts, tq, tk, put, step == 0)
-            return carry
-
-        lax.fori_loop(0, tiles, maps_tile, 0)
-        exchange(2 * step, source, target, stride, stride)
-
-        def value(v, t):
-            return target[pl.ds(t * stride + v, ROWS, stride=depth * stride), :]
-
-        def coef(v, t):
-            return got1[pl.ds(t * COEFS + v, ROWS, stride=depth * COEFS), :]
-
-        def pin(side, component):
-            lanes = pl.ds(pl.multiple_of((chip // ROWS) * LANES, LANES), LANES)
-            sub = lax.broadcasted_iota(jnp.int32, (ROWS, LANES), 0)
-            return jnp.sum(jnp.where(sub == chip % ROWS, pins[side, component, :, lanes], 0.0), axis=0, keepdims=True)
-
-        def put_wave(v, t, value):
-            back[pl.ds(t * WAVES + v, ROWS, stride=depth * WAVES), :] = value
-
-        owner_solve(chips, thick, value, coef, pin, put_wave)
-        wave = waves.at[step]
-        exchange(2 * step + 1, back, wave, WAVES, WAVES)
-
-        def solve_tile(tile, carry):
-            lanes = pl.ds(pl.multiple_of(tile * LANES, LANES), LANES)
-
-            def get(v):
-                return wave[pl.ds(tile * (ROWS * WAVES) + v, ROWS, stride=WAVES), :]
-
-            solved_fields(thick, lanes, m, a, f, tp, ts, tq, get, edge)
-            return carry
-
-        lax.fori_loop(0, tiles, solve_tile, 0)
-        borders = [
-            pltpu.make_async_remote_copy(
-                src_ref=edge.at[k],
-                dst_ref=halo.at[step, 1 - k],
-                send_sem=edge_send.at[2 * step + k],
-                recv_sem=edge_recv.at[2 * step + k],
-                device_id=neighbour,
-                device_id_type=MESH,
-            )
-            for k, neighbour in enumerate((low, high))
-        ]
-        for copy in borders:
-            copy.start()
-        for copy in borders:
-            copy.wait()
-        if step < STEPS - 1:
-            torque(0, thick, f, a, halo.at[step], m)
-
-    out_far = pltpu.make_async_remote_copy(
-        src_ref=m.at[:, other_planes],
-        dst_ref=out_hbm.at[:, :, mine_rows],
-        send_sem=out_send,
-        recv_sem=out_recv,
-        device_id=(partner, group),
-        device_id_type=MESH,
-    )
+
     out_here = pltpu.make_async_copy(m.at[:, mine_planes], out_hbm.at[:, :, mine_rows], out_sem)
-    torque(other * half, half, f, a, halo.at[STEPS - 1], m)
-    out_far.start()
+    for part in range(half // 8):
+        torque(other * half + part * 8, 8, f, a, halo.at[STEPS - 1], m)
+        far_part(part).start()
     torque(core * half, half, f, a, halo.at[STEPS - 1], m)
     out_here.start()
+    for step in range(STEPS):
+        sent = (send1, send2)[step]
+        rows = pl.ds(0, (chips - 1) * (COEFS, WAVES)[step])
+        pltpu.make_async_copy(sent.at[rows], sent.at[rows], map_send.at[step]).wait()
+        rows = pl.ds(0, (chips - 1) * WAVES)
+        pltpu.make_async_copy(back.at[step, rows], back.at[step, rows], wave_send.at[step]).wait()
+        for side in range(2):
+            pltpu.make_async_copy(edge.at[step, side], edge.at[step, side], edge_send.at[2 * step + side]).wait()
     out_here.wait()
-    out_far.wait()
+    for part in range(half // 8):
+        far_part(part).wait()
 
 
 def per_device(chips, ring, groups, magnetization, easy_axes, pins):
     _, half, rows, wide = magnetization.shape
     thick = 2 * half
     blocks = chips * WAVES
+    tiles = wide // LANES
     f32 = jnp.float32
     any_space = pl.BlockSpec(memory_space=pl.ANY)
     dma = pltpu.SemaphoreType.DMA
     return pl.pallas_call(
         functools.partial(kernel, chips, ring, groups),
         out_shape=jax.ShapeDtypeStruct(magnetization.shape, f32),
-        in_specs=[any_space] * 3,
+        in_specs=[pl.BlockSpec(memory_space=pltpu.HBM)] * 3,
         out_specs=any_space,
         scratch_shapes=[
             pltpu.VMEM((3, thick, ROWS, wide), f32),
@@ -497,28 +534,30 @@
             pltpu.VMEM((chips * COEFS, LANES), f32),
             pltpu.VMEM((blocks, LANES), f32),
             pltpu.VMEM((blocks, LANES), f32),
-            pltpu.VMEM((blocks, LANES), f32),
             pltpu.VMEM((STEPS, blocks, LANES), f32),
-            pltpu.VMEM((2, 3, thick, wide), f32),
-            pltpu.VMEM((STEPS, 2, 3, thick, wide), f32),
+            pltpu.VMEM((STEPS, blocks, LANES), f32),
+            pltpu.VMEM((STEPS, 2, tiles, 3, thick, LANES), f32),
+            pltpu.VMEM((STEPS, 2, tiles, 3, thick, LANES), f32),
             dma((3,)),
-            dma((2,)),
-            dma((2,)),
-            dma((2 * STEPS,)),
-            dma((2 * STEPS,)),
+            dma((2 * tiles,)),
+            dma((2 * tiles,)),
+            dma((STEPS,)),
+            dma((STEPS,)),
+            dma((STEPS,)),
+            dma((STEPS * tiles,)),
             dma((2 * STEPS,)),
             dma((2 * STEPS,)),
             dma,
-            dma,
-            dma,
+            dma((half // 8,)),
+            dma((half // 8,)),
         ],
-        compiler_params=pltpu.CompilerParams(collective_id=0, has_side_effects=True),
-    )(magnetization, easy_axes, pins)
+        compiler_params=pltpu.CompilerParams(collective_id=0, has_side_effects=True, vmem_limit_bytes=20 * 2**20),
+    )(*(pltpu.with_memory_space_constraint(x, pltpu.HBM) for x in (magnetization, easy_axes, pins)))
 
 
 def solution(mesh):
     chips, groups = mesh.shape["gx"] // 2, mesh.shape["gy"]
-    body = functools.partial(per_device, chips, 8 if chips % 8 == 0 else 1, groups)
+    body = functools.partial(per_device, chips, ROWS, groups)
     spec = P(None, "gx", "gy", None)
     return jax.shard_map(
         body, mesh=mesh, in_specs=(spec, spec, P(None, None, "gy", None)), out_specs=spec, check_vma=False

time: 71.3 us -> 60.8 us (0.85)
  Pallas kernels: 68.3 us -> 59.5 us
  local copies, waits for them, and re-layouts: 2.77 us -> 1.15 us
    pallas_call x1, Pallas kernels: 68.3 us -> 59.5 us  [per_device(): pl.pallas_call(functools.partial(kernel, chips, ring, groups), out_shape=...]
    unnamed x1, local copies, waits for them, and re-layouts: 2.77 us -> 1.15 us
where the time goes in v2:
time: 60.8 us; the launch traced here: 60.7 us
  Pallas kernels  59.5 us (98%)
  local copies, waits for them, and re-layouts  1.15 us (2%)
    pallas_call x1, Pallas kernels, per_device(): pl.pallas_call(functools.partial(kernel, chips, ring, groups), out_shape=...  59.5 us

profile of v2, /device:TPU:1, one launch (start us, length us, event | category | flops | bytes accessed | tf_op | source)
XLA Modules:
  0.0 60.7 jit_solution(13326533665489238238)
XLA Ops:
  0.0 59.5 %shard_map.37 = f32[3,16,16,512]{3,2,1,0:T(8,128)S(1)} custom-call(f32[3,16,16,512]{3,2,1,0:T(8,128)} %m_hbm.1, f32[3,16,16,512]{3,2,1,0:T(8,128)} %a_hbm.1, f32[2,3,16,512]{3,2,1,0:T(8,128)} %pins_hbm.1), custom_call_target="tpu_custom_call" | custom-call | tf_op jit(solution)/shard_map/pallas_call | solution.py:519
  59.5 1.1 %copy.5 = f32[3,16,16,512]{3,2,1,0:T(8,128)} copy(f32[3,16,16,512]{3,2,1,0:T(8,128)S(1)} %shard_map.37) | data formatting | bytes 3145728

commit v3 on v2

--- a/solution.py
+++ b/solution.py
@@ -14,6 +14,7 @@
 ROWS = 8
 COEFS = 16
 WAVES = 8
+KEPT = 6
 
 diffusion = 4000.0
 anisotropy_rate = 0.3
@@ -36,13 +37,13 @@
     return lax.fori_loop(0, count // unroll, chunk, carry)
 
 
-def wave_maps(thick, lanes, m, a, tp, ts, tq, tk, put, with_coefs):
+def wave_maps(thick, rows, lanes, m, a, tp, ts, tq, tk, put, with_coefs):
     zero = jnp.zeros((ROWS, LANES), jnp.float32)
     r2 = decay * decay
     rate = anisotropy_rate
 
     def load(ref, i):
-        return tuple(ref[c, i, :, lanes] for c in range(3))
+        return tuple(ref[c, i, rows, lanes] for c in range(3))
 
     def up1(base, k, p):
         i = base + k
@@ -86,7 +87,7 @@
     def up2(base, k, carry):
         i = base + k
         p2, l3, r3, w, pk, sk, h23, sum23, l3p, l3s, r3p, r3s = carry
-        m3 = m[2, i, :, lanes]
+        m3 = m[2, i, rows, lanes]
         a1, a2, a3 = load(a, i)
         p2 = decay * p2 + ts[i]
         f2 = p2 + tq[i]
@@ -131,7 +132,35 @@
         put(15, across * r3s)
 
 
-def solved_fields(thick, lanes, m, a, f, tp, ts, tq, get, first, last):
+def merged_maps(half, first, second, put):
+    hop = decay**half
+    square = hop * hop
+    l1, r1 = first(0), second(1)
+    put(0, hop * l1 + second(0))
+    put(1, first(1) + hop * r1)
+    alpha0, beta0, gamma0 = first(6), first(7), first(8)
+    alpha1, beta1, gamma1 = second(6), second(7), second(8)
+    l2 = first(2) + gamma0 * r1
+    r2 = second(3) + alpha1 * l1
+    put(2, hop * l2 + second(2) + beta1 * l1)
+    put(3, first(3) + beta0 * r1 + hop * r2)
+    put(6, alpha0 + square * alpha1)
+    put(7, hop * (beta0 + beta1))
+    put(8, square * gamma0 + gamma1)
+    a0, b0, g0 = first(9), first(10), first(11)
+    a1, b1, g1 = second(9), second(10), second(11)
+    put(4, hop * (first(4) + first(13) * r1 + g0 * r2) + second(4) + second(12) * l1 + b1 * l2)
+    put(5, first(5) + first(15) * r1 + b0 * r2 + hop * (second(5) + second(14) * l1 + a1 * l2))
+    put(9, a0 + square * a1)
+    put(10, hop * (b0 + b1))
+    put(11, square * g0 + g1)
+    put(12, hop * (first(12) + hop * g0 * alpha1 + second(12)) + b1 * beta0)
+    put(13, hop * (hop * first(13) + g0 * beta1 + b1 * gamma0) + second(13))
+    put(14, first(14) + hop * (b0 * alpha1 + hop * second(14) + a1 * beta0))
+    put(15, hop * (first(15) + second(15) + hop * a1 * gamma0) + b0 * beta1)
+
+
+def solved_fields(thick, lanes, m, a, f, tp, ts, tq, get):
     rate = anisotropy_rate
 
     def load(ref, i):
@@ -139,8 +168,6 @@
 
     def keep(c, base, k, value):
         f[c, base + k, :, lanes] = value
-        first.at[c, pl.ds(base, 8)][k : k + 1] = value[0:1]
-        last.at[c, pl.ds(base, 8)][k : k + 1] = value[ROWS - 1 : ROWS]
 
     def up1(base, k, p):
         i = base + k
@@ -275,22 +302,23 @@
 
     def chunk(step, carry):
         base = pl.multiple_of(planes_from + step * 8, 8)
-        rows = [
-            [jnp.concatenate([halo[side, t, c, pl.ds(base, 8)] for t in range(wide // LANES)], axis=1) for c in range(3)]
-            for side in range(2)
-        ]
         for k in range(8):
-            plane(base + k, k, rows)
+            plane(base + k)
         return carry
 
-    def plane(i, k, rows):
+    def border(c, i, side):
+        row = side * (wide // LANES)
+        parts = [jnp.broadcast_to(halo[c, i, row + t : row + t + 1], (ROWS, LANES)) for t in range(wide // LANES)]
+        return jnp.concatenate(parts, axis=1)
+
+    def plane(i):
         field = [f[c, i] for c in range(3)]
         axes = [a[c, i] for c in range(3)]
         projection = field[0] * axes[0] + field[1] * axes[1] + field[2] * axes[2]
         effective = []
         for c in range(3):
-            low = jnp.where(sub == 0, rows[0][c][k : k + 1], pltpu.roll(field[c], 1, 0))
-            high = jnp.where(sub == ROWS - 1, rows[1][c][k : k + 1], pltpu.roll(field[c], ROWS - 1, 0))
+            low = jnp.where(sub == 0, border(c, i, 0), pltpu.roll(field[c], 1, 0))
+            high = jnp.where(sub == ROWS - 1, border(c, i, 1), pltpu.roll(field[c], ROWS - 1, 0))
             sides = low + high + pltpu.roll(field[c], 1, 1) + pltpu.roll(field[c], wide - 1, 1)
             effective.append(exchange_rate * (sides - 4.0 * field[c]) + projection * axes[c])
         rotated = []
@@ -308,121 +336,169 @@
 def kernel(
     chips, ring, groups,
     m_hbm, a_hbm, pins_hbm, out_hbm,
-    m, a, f, pins, tp, ts, tq, tk, send1, got1, send2, got2, back, waves, edge, halo,
-    load_sem, swap_send, swap_recv, map_send, map_recv, wave_send, wave_recv, edge_send, edge_recv, out_sem, out_send, out_recv,
+    m, a, f, own_m, own_a, pins, tp, ts, tq, tk, blocks, send1, got1, send2, got2, back, waves, side_m, side_a, side_f, side_waves,
+    load_sem, swap_send, swap_recv, block_send, block_recv, map_send, map_recv, wave_send, wave_recv, side_send, side_recv, border_send, border_recv, out_sem, out_send, out_recv,
 ):
     position, group = lax.axis_index("gx"), lax.axis_index("gy")
-    chip, core = position // 2, position % 2
+    chip, core = lax.div(position, 2), lax.rem(position, 2)
     other = 1 - core
     partner = chip * 2 + other
     half = m_hbm.shape[1]
     thick = 2 * half
     tiles = m.shape[-1] // LANES
-    here = chip // ring
-    low = (partner, (group + groups - other) % groups)
-    high = (partner, (group + core) % groups)
+    here, there = lax.div(chip, ring), lax.rem(chip, ring)
+    low = (partner, lax.rem(group + groups - other, groups))
+    high = (partner, lax.rem(group + core, groups))
     mine_rows = pl.ds(pl.multiple_of(core * ROWS, ROWS), ROWS)
     other_rows = pl.ds(pl.multiple_of(other * ROWS, ROWS), ROWS)
     mine_planes = pl.ds(core * half, half)
     other_planes = pl.ds(other * half, half)
 
     loads = [
-        pltpu.make_async_copy(a_hbm.at[:, :, mine_rows], a.at[:, mine_planes], load_sem.at[0]),
-        pltpu.make_async_copy(m_hbm.at[:, :, mine_rows], m.at[:, mine_planes], load_sem.at[1]),
+        pltpu.make_async_copy(a_hbm, own_a, load_sem.at[0]),
+        pltpu.make_async_copy(m_hbm, own_m, load_sem.at[1]),
         pltpu.make_async_copy(pins_hbm.at[:, :, mine_rows], pins, load_sem.at[2]),
+        pltpu.make_async_copy(a_hbm.at[:, :, mine_rows], a.at[:, mine_planes], load_sem.at[3]),
+        pltpu.make_async_copy(m_hbm.at[:, :, mine_rows], m.at[:, mine_planes], load_sem.at[4]),
     ]
 
-    def zigzag(k):
-        return ((k + 1) // 2) * (2 * ((k + 1) % 2) - 1)
+    def outward(count):
+        return [count // 2 + ((k + 1) // 2) * (2 * ((k + 1) % 2) - 1) for k in range(count)]
+
+    far_rows = [lax.rem(there + k, ring) for k in outward(ring)]
+    far_tiles = [lax.rem(here + k, tiles) for k in outward(tiles)]
+    peers = [(tile * ring + row) * 2 + core for row in far_rows for tile in far_tiles][:-1]
 
     def far_tile(j):
-        return (here + tiles // 2 + zigzag(j)) % tiles
-
-    def far_chip(tile, k):
-        return tile * ring + (chip % ring + ring // 2 + zigzag(k)) % ring
-
-    def peer(t):
-        return far_chip(far_tile(t % tiles), t // tiles)
+        turn = lax.div(j + 1, 2) * (2 * lax.rem(j + 1, 2) - 1)
+        return lax.rem(here + tiles // 2 + tiles + turn, tiles)
 
     def lanes_of(tile):
         return pl.ds(pl.multiple_of(tile * LANES, LANES), LANES)
 
     barrier = pltpu.get_barrier_semaphore()
-
-    def greet(t, carry):
-        pl.semaphore_signal(barrier, inc=1, device_id=(peer(t) * 2 + core, group), device_id_type=MESH)
-        return carry
-
-    lax.fori_loop(0, chips - 1, greet, 0)
+    for to in peers:
+        pl.semaphore_signal(barrier, inc=1, device_id=(to, group), device_id_type=MESH)
     for neighbour in (low, high):
         pl.semaphore_signal(barrier, inc=1, device_id=neighbour, device_id_type=MESH)
     for copy in loads:
         copy.start()
+    for copy in loads[:2]:
+        copy.wait()
+
+    for where, rows in ((2, other_rows), (core, mine_rows)):
+
+        def own_tile(tile, carry):
+            def put(v, value):
+                blocks[where, tile, v] = value
+
+            wave_maps(half, rows, lanes_of(tile), own_m, own_a, tp, ts, tq, tk, put, True)
+            return carry
+
+        lax.fori_loop(0, tiles, own_tile, 0)
     pl.semaphore_wait(barrier, chips + 1)
 
-    def swaps(j):
-        lanes = lanes_of(far_tile(j))
+    def give_block(j):
+        tile = far_tile(j)
+        return pltpu.make_async_remote_copy(
+            src_ref=blocks.at[2, tile],
+            dst_ref=blocks.at[core, tile],
+            send_sem=block_send.at[j],
+            recv_sem=block_recv.at[j],
+            device_id=(partner, group),
+            device_id_type=MESH,
+        )
+
+    def start_block(j, carry):
+        give_block(j).start()
+        return carry
+
+    lax.fori_loop(0, tiles, start_block, 0)
+    swaps = [
+        pltpu.make_async_remote_copy(
+            src_ref=hbm.at[:, :, other_rows],
+            dst_ref=vmem.at[:, mine_planes],
+            send_sem=swap_send.at[k],
+            recv_sem=swap_recv.at[k],
+            device_id=(partner, group),
+            device_id_type=MESH,
+        )
+        for k, (hbm, vmem) in enumerate(((a_hbm, a), (m_hbm, m)))
+    ]
+
+    def borders(number, source, target):
         return [
             pltpu.make_async_remote_copy(
-                src_ref=hbm.at[:, :, other_rows, lanes],
-                dst_ref=vmem.at[:, mine_planes, :, lanes],
-                send_sem=swap_send.at[2 * j + k],
-                recv_sem=swap_recv.at[2 * j + k],
-                device_id=(partner, group),
+                src_ref=source.at[:, :, (0, ROWS - 1)[k], t * LANES : (t + 1) * LANES],
+                dst_ref=target.at[:, :, (1 - k) * tiles + t],
+                send_sem=border_send.at[number],
+                recv_sem=border_recv.at[number],
+                device_id=(low, high)[k],
                 device_id_type=MESH,
             )
-            for k, (hbm, vmem) in enumerate(((a_hbm, a), (m_hbm, m)))
+            for k in range(2)
+            for t in range(tiles)
         ]
-
-    def start_swap(j, carry):
-        for copy in swaps(j):
-            copy.start()
-        return carry
-
-    lax.fori_loop(0, tiles, start_swap, 0)
-    for copy in loads:
-        copy.wait()
 
     depth = chips // ROWS
     for step in range(STEPS):
-        source, target, stride = (send1, got1, COEFS) if step == 0 else (send2, got2, WAVES)
-
-        def block(number, stride):
-            return pl.ds(pl.multiple_of(number * stride, 8), stride)
-
-        def message(source, target, stride, to, sends, recvs):
+        source, target, stride, size = (send1, got1, COEFS, COEFS) if step == 0 else (send2, got2, WAVES, KEPT)
+
+        def block(number, stride, size):
+            return pl.ds(pl.multiple_of(number * stride, 8), size)
+
+        def message(source, target, stride, size, to, sends, recvs):
             return pltpu.make_async_remote_copy(
-                src_ref=source.at[block(to, stride)],
-                dst_ref=target.at[block(chip, stride)],
+                src_ref=source.at[block(to, stride, size)],
+                dst_ref=target.at[block(chip, stride, size)],
                 send_sem=sends,
                 recv_sem=recvs,
                 device_id=(to * 2 + core, group),
                 device_id_type=MESH,
             )
 
-        def own_message(source, target, stride, recvs):
-            return pltpu.make_async_copy(source.at[block(chip, stride)], target.at[block(chip, stride)], recvs)
+        def own_message(source, target, stride, size, recvs):
+            own = block(chip, stride, size)
+            return pltpu.make_async_copy(source.at[own], target.at[own], recvs)
+
+        def wait_rows(ref, count, sem):
+            rows = pl.ds(0, count)
+            pltpu.make_async_copy(ref.at[rows], ref.at[rows], sem).wait()
 
         def maps_tile(j, carry):
             tile = far_tile(j)
-            if step == 0:
-                for copy in swaps(j):
-                    copy.wait()
 
             def put(v, value):
                 source[pl.ds(tile * (ROWS * stride) + v, ROWS, stride=stride), :] = value
 
-            wave_maps(thick, lanes_of(tile), m, a, tp, ts, tq, tk, put, step == 0)
-
-            def start(k, carry):
-                message(source, target, stride, far_chip(tile, k), map_send.at[step], map_recv.at[step]).start()
-                return carry
-
-            return lax.fori_loop(0, ring - (j + 1) // tiles, start, carry)
+            if step == 0:
+                give_block(j).wait()
+                merged_maps(half, lambda v: blocks[0, tile, v], lambda v: blocks[1, tile, v], put)
+            else:
+                wave_maps(thick, slice(None), lanes_of(tile), m, a, tp, ts, tq, tk, put, False)
+            for k, row in enumerate(far_rows):
+                copy = message(source, target, stride, size, tile * ring + row, map_send.at[step], map_recv.at[step])
+                if k < ring - 1:
+                    copy.start()
+                else:
+                    pl.when(j < tiles - 1)(copy.start)
+            return carry
 
         lax.fori_loop(0, tiles, maps_tile, 0)
-        own_message(source, target, stride, map_recv.at[step]).start()
-        pltpu.make_async_copy(source, target, map_recv.at[step]).wait()
+        own_message(source, target, stride, size, map_recv.at[step]).start()
+        if step == 0:
+            for copy in swaps:
+                copy.start()
+            for copy in loads[2:]:
+                copy.wait()
+            for copy in swaps:
+                copy.wait()
+            for copy in borders(0, m, side_m.at[0]) + borders(STEPS, a, side_a):
+                copy.start()
+        if step > 0:
+            for copy in borders(step, m, side_m.at[step]):
+                copy.start()
+        wait_rows(target, chips * size, map_recv.at[step])
 
         def value(v, t):
             return target[pl.ds(t * stride + v, ROWS, stride=depth * stride), :]
@@ -433,7 +509,7 @@
         def pin(side, component):
             sub = lax.broadcasted_iota(jnp.int32, (ROWS, LANES), 0)
             row = pins[side, component, :, lanes_of(here)]
-            return jnp.sum(jnp.where(sub == chip % ROWS, row, 0.0), axis=0, keepdims=True)
+            return jnp.sum(jnp.where(sub == there, row, 0.0), axis=0, keepdims=True)
 
         out_waves, wave = back.at[step], waves.at[step]
 
@@ -442,41 +518,41 @@
 
         owner_solve(chips, thick, value, coef, pin, put_wave)
 
-        def send_wave(t, carry):
-            message(out_waves, wave, WAVES, peer(t), wave_send.at[step], wave_recv.at[step * tiles + here]).start()
-            return carry
-
-        lax.fori_loop(0, chips - 1, send_wave, 0)
-        own_message(out_waves, wave, WAVES, wave_recv.at[step * tiles + here]).start()
-
-        def border(side, tile):
-            return pltpu.make_async_remote_copy(
-                src_ref=edge.at[step, side, tile],
-                dst_ref=halo.at[step, 1 - side, tile],
-                send_sem=edge_send.at[2 * step + side],
-                recv_sem=edge_recv.at[2 * step + 1 - side],
-                device_id=(low, high)[side],
-                device_id_type=MESH,
-            )
-
-        def solve_tile(j, carry):
-            tile = far_tile(tiles - 1 - j)
-            rows = pl.ds(pl.multiple_of(tile * (ring * WAVES), 8), ring * WAVES)
-            pltpu.make_async_copy(out_waves.at[rows], wave.at[rows], wave_recv.at[step * tiles + tile]).wait()
-
+        for to in peers:
+            message(out_waves, wave, WAVES, KEPT, lax.div(to, 2), wave_send.at[step], wave_recv.at[step]).start()
+        own_message(out_waves, wave, WAVES, KEPT, wave_recv.at[step]).start()
+        wait_rows(wave, chips * KEPT, wave_recv.at[step])
+
+        for k, row in enumerate((0, ring - 1)):
+            for tile in range(tiles):
+                pltpu.make_async_remote_copy(
+                    src_ref=wave.at[block(tile * ring + row, WAVES, KEPT)],
+                    dst_ref=side_waves.at[step, block((1 - k) * tiles + tile, WAVES, KEPT)],
+                    send_sem=side_send.at[step],
+                    recv_sem=side_recv.at[step],
+                    device_id=(low, high)[k],
+                    device_id_type=MESH,
+                ).start()
+
+        def solve_tile(tile, carry):
             def get(v):
                 return wave[pl.ds(tile * (ROWS * WAVES) + v, ROWS, stride=WAVES), :]
 
-            solved_fields(thick, lanes_of(tile), m, a, f, tp, ts, tq, get, edge.at[step, 0, tile], edge.at[step, 1, tile])
-            for side in range(2):
-                border(side, tile).start()
+            solved_fields(thick, lanes_of(tile), m, a, f, tp, ts, tq, get)
             return carry
 
         lax.fori_loop(0, tiles, solve_tile, 0)
-        for side in range(2):
-            pltpu.make_async_copy(edge.at[step, side], halo.at[step, side], edge_recv.at[2 * step + side]).wait()
+        for number, target in ((step, side_m.at[step]), (STEPS, side_a))[: STEPS - step]:
+            pltpu.make_async_copy(target, target, border_recv.at[number]).wait()
+            pltpu.make_async_copy(target, target, border_send.at[number]).wait()
+        wait_rows(side_waves.at[step], ROWS * KEPT, side_recv.at[step])
+
+        def side_wave(v):
+            return side_waves[step, pl.ds(v, ROWS, stride=WAVES), :]
+
+        solved_fields(thick, slice(None), side_m.at[step], side_a, side_f, tp, ts, tq, side_wave)
         if step < STEPS - 1:
-            torque(0, thick, f, a, halo.at[step], m)
+            torque(0, thick, f, a, side_f, m)
 
     def far_part(part):
         planes = pl.ds(other * half + part * 8, 8)
@@ -491,18 +567,14 @@
 
     out_here = pltpu.make_async_copy(m.at[:, mine_planes], out_hbm.at[:, :, mine_rows], out_sem)
     for part in range(half // 8):
-        torque(other * half + part * 8, 8, f, a, halo.at[STEPS - 1], m)
+        torque(other * half + part * 8, 8, f, a, side_f, m)
         far_part(part).start()
-    torque(core * half, half, f, a, halo.at[STEPS - 1], m)
+    torque(core * half, half, f, a, side_f, m)
     out_here.start()
     for step in range(STEPS):
-        sent = (send1, send2)[step]
-        rows = pl.ds(0, (chips - 1) * (COEFS, WAVES)[step])
-        pltpu.make_async_copy(sent.at[rows], sent.at[rows], map_send.at[step]).wait()
-        rows = pl.ds(0, (chips - 1) * WAVES)
-        pltpu.make_async_copy(back.at[step, rows], back.at[step, rows], wave_send.at[step]).wait()
-        for side in range(2):
-            pltpu.make_async_copy(edge.at[step, side], edge.at[step, side], edge_send.at[2 * step + side]).wait()
+        wait_rows((send1, send2)[step], (chips - 1) * (COEFS, KEPT)[step], map_send.at[step])
+        wait_rows(back.at[step], (chips - 1) * KEPT, wave_send.at[step])
+        wait_rows(side_waves.at[step], ROWS * KEPT, side_send.at[step])
     out_here.wait()
     for part in range(half // 8):
         far_part(part).wait()
@@ -525,28 +597,37 @@
             pltpu.VMEM((3, thick, ROWS, wide), f32),
             pltpu.VMEM((3, thick, ROWS, wide), f32),
             pltpu.VMEM((3, thick, ROWS, wide), f32),
+            pltpu.VMEM(magnetization.shape, f32),
+            pltpu.VMEM(magnetization.shape, f32),
             pltpu.VMEM((2, 3, ROWS, wide), f32),
             pltpu.VMEM((thick, ROWS, LANES), f32),
             pltpu.VMEM((thick, ROWS, LANES), f32),
             pltpu.VMEM((thick, ROWS, LANES), f32),
             pltpu.VMEM((thick, ROWS, LANES), f32),
+            pltpu.VMEM((3, tiles, COEFS, ROWS, LANES), f32),
             pltpu.VMEM((chips * COEFS, LANES), f32),
             pltpu.VMEM((chips * COEFS, LANES), f32),
             pltpu.VMEM((blocks, LANES), f32),
             pltpu.VMEM((blocks, LANES), f32),
             pltpu.VMEM((STEPS, blocks, LANES), f32),
             pltpu.VMEM((STEPS, blocks, LANES), f32),
-            pltpu.VMEM((STEPS, 2, tiles, 3, thick, LANES), f32),
-            pltpu.VMEM((STEPS, 2, tiles, 3, thick, LANES), f32),
-            dma((3,)),
-            dma((2 * tiles,)),
-            dma((2 * tiles,)),
+            pltpu.VMEM((STEPS, 3, thick, ROWS, LANES), f32),
+            pltpu.VMEM((3, thick, ROWS, LANES), f32),
+            pltpu.VMEM((3, thick, ROWS, LANES), f32),
+            pltpu.VMEM((STEPS, ROWS * WAVES, LANES), f32),
+            dma((5,)),
+            dma((2,)),
+            dma((2,)),
+            dma((tiles,)),
+            dma((tiles,)),
             dma((STEPS,)),
             dma((STEPS,)),
             dma((STEPS,)),
-            dma((STEPS * tiles,)),
-            dma((2 * STEPS,)),
-            dma((2 * STEPS,)),
+            dma((STEPS,)),
+            dma((STEPS,)),
+            dma((STEPS,)),
+            dma((STEPS + 1,)),
+            dma((STEPS + 1,)),
             dma,
             dma((half // 8,)),
             dma((half // 8,)),

time: 60.8 us -> 56 us (0.921)
  Pallas kernels: 59.5 us -> 54.7 us
    pallas_call x1, Pallas kernels: 59.5 us -> 54.7 us  [per_device(): pl.pallas_call(functools.partial(kernel, chips, ring, groups), out_shape=...]
where the time goes in v3:
time: 56 us; the launch traced here: 55.9 us
  Pallas kernels  54.7 us (98%)
  local copies, waits for them, and re-layouts  1.15 us (2%)
    pallas_call x1, Pallas kernels, per_device(): pl.pallas_call(functools.partial(kernel, chips, ring, groups), out_shape=...  54.7 us
    unnamed x1, local copies, waits for them, and re-layouts  1.15 us

profile of v3, /device:TPU:1, one launch (start us, length us, event | category | flops | bytes accessed | tf_op | source)
XLA Modules:
  0.0 55.9 jit_solution(12473663607203082981)
XLA Ops:
  0.0 54.7 %shard_map.37 = f32[3,16,16,512]{3,2,1,0:T(8,128)S(1)} custom-call(f32[3,16,16,512]{3,2,1,0:T(8,128)} %m_hbm.1, f32[3,16,16,512]{3,2,1,0:T(8,128)} %a_hbm.1, f32[2,3,16,512]{3,2,1,0:T(8,128)} %pins_hbm.1), custom_call_target="tpu_custom_call" | custom-call | tf_op jit(solution)/shard_map/pallas_call | solution.py:591
  54.7 1.1 %copy.5 = f32[3,16,16,512]{3,2,1,0:T(8,128)} copy(f32[3,16,16,512]{3,2,1,0:T(8,128)S(1)} %shard_map.37) | data formatting | bytes 3145728

commit v4 on v3

--- a/solution.py
+++ b/solution.py
@@ -15,6 +15,7 @@
 COEFS = 16
 WAVES = 8
 KEPT = 6
+PART = 4
 
 diffusion = 4000.0
 anisotropy_rate = 0.3
@@ -27,7 +28,9 @@
 weight = 1.0 / (diffusion * (1.0 / decay - decay))
 
 
-def sweep(count, carry, body, reverse=False, unroll=8):
+def sweep(count, carry, body, reverse=False, unroll=32):
+    unroll = min(unroll, count)
+
     def chunk(step, carry):
         base = pl.multiple_of((count // unroll - 1 - step if reverse else step) * unroll, unroll)
         for k in reversed(range(unroll)) if reverse else range(unroll):
@@ -113,7 +116,7 @@
 
     one = jnp.ones((ROWS, LANES), jnp.float32)
     p2, l3, r3, _, _, gamma12, h23, sum23, l3p, l3s, r3p, r3s = sweep(
-        thick, (zero, zero, zero, one) + (zero,) * 8, up2, unroll=4
+        thick, (zero, zero, zero, one) + (zero,) * 8, up2, unroll=8
     )
     put(2, p2)
     put(4, l3)
@@ -300,10 +303,11 @@
     wide = f.shape[-1]
     sub = lax.broadcasted_iota(jnp.int32, (ROWS, wide), 0)
 
+    group = min(16, planes)
+
     def chunk(step, carry):
-        base = pl.multiple_of(planes_from + step * 8, 8)
-        for k in range(8):
-            plane(base + k)
+        for k in range(group):
+            plane(planes_from + step * group + k)
         return carry
 
     def border(c, i, side):
@@ -330,7 +334,7 @@
         for c in range(3):
             out[c, i] = rotated[c] * scale
 
-    lax.fori_loop(0, planes // 8, chunk, 0)
+    lax.fori_loop(0, planes // group, chunk, 0)
 
 
 def kernel(
@@ -555,10 +559,10 @@
             torque(0, thick, f, a, side_f, m)
 
     def far_part(part):
-        planes = pl.ds(other * half + part * 8, 8)
+        planes = pl.ds(other * half + part * PART, PART)
         return pltpu.make_async_remote_copy(
             src_ref=m.at[:, planes],
-            dst_ref=out_hbm.at[:, pl.ds(part * 8, 8), mine_rows],
+            dst_ref=out_hbm.at[:, pl.ds(part * PART, PART), mine_rows],
             send_sem=out_send.at[part],
             recv_sem=out_recv.at[part],
             device_id=(partner, group),
@@ -566,8 +570,8 @@
         )
 
     out_here = pltpu.make_async_copy(m.at[:, mine_planes], out_hbm.at[:, :, mine_rows], out_sem)
-    for part in range(half // 8):
-        torque(other * half + part * 8, 8, f, a, side_f, m)
+    for part in range(half // PART):
+        torque(other * half + part * PART, PART, f, a, side_f, m)
         far_part(part).start()
     torque(core * half, half, f, a, side_f, m)
     out_here.start()
@@ -576,7 +580,7 @@
         wait_rows(back.at[step], (chips - 1) * KEPT, wave_send.at[step])
         wait_rows(side_waves.at[step], ROWS * KEPT, side_send.at[step])
     out_here.wait()
-    for part in range(half // 8):
+    for part in range(half // PART):
         far_part(part).wait()
 
 
@@ -629,8 +633,8 @@
             dma((STEPS + 1,)),
             dma((STEPS + 1,)),
             dma,
-            dma((half // 8,)),
-            dma((half // 8,)),
+            dma((half // PART,)),
+            dma((half // PART,)),
         ],
         compiler_params=pltpu.CompilerParams(collective_id=0, has_side_effects=True, vmem_limit_bytes=20 * 2**20),
     )(*(pltpu.with_memory_space_constraint(x, pltpu.HBM) for x in (magnetization, easy_axes, pins)))

time: 56 us -> 54.5 us (0.973)
  Pallas kernels: 54.7 us -> 53.2 us
    pallas_call x1, Pallas kernels: 54.7 us -> 53.2 us  [per_device(): pl.pallas_call(functools.partial(kernel, chips, ring, groups), out_shape=...]
where the time goes in v4:
time: 54.5 us; the launch traced here: 54.4 us
  Pallas kernels  53.2 us (98%)
  local copies, waits for them, and re-layouts  1.15 us (2%)
    pallas_call x1, Pallas kernels, per_device(): pl.pallas_call(functools.partial(kernel, chips, ring, groups), out_shape=...  53.2 us
    unnamed x1, local copies, waits for them, and re-layouts  1.15 us

profile of v4, /device:TPU:1, one launch (start us, length us, event | category | flops | bytes accessed | tf_op | source)
XLA Modules:
  0.0 54.4 jit_solution(16987866097579112536)
XLA Ops:
  0.0 53.2 %shard_map.37 = f32[3,16,16,512]{3,2,1,0:T(8,128)S(1)} custom-call(f32[3,16,16,512]{3,2,1,0:T(8,128)} %m_hbm.1, f32[3,16,16,512]{3,2,1,0:T(8,128)} %a_hbm.1, f32[2,3,16,512]{3,2,1,0:T(8,128)} %pins_hbm.1), custom_call_target="tpu_custom_call" | custom-call | tf_op jit(solution)/shard_map/pallas_call | solution.py:595
  53.2 1.1 %copy.5 = f32[3,16,16,512]{3,2,1,0:T(8,128)} copy(f32[3,16,16,512]{3,2,1,0:T(8,128)S(1)} %shard_map.37) | data formatting | bytes 3145728
